TPU v7x, 128 devices: a whole 4x4x4 slice. The times are simulated.
128 devices in a mesh: gx: 4 (over z_lo, core), gy: 4 (over x), gz: 8 (over y, z_hi).
Axes of the slice: x: 4, y: 4, z: 4 (z_hi: 2, z_lo: 2; z = z_hi * 2 + z_lo), core: 2. Of those that a mesh axis runs over, the one named last changes fastest.
Arguments:
- positions: float32 [4, 4, 8, 3, 256], P('gx', 'gy', 'gz'), may hold values from 0 to 1
- species: int32 [4, 4, 8, 256], P('gx', 'gy', 'gz'), may hold values from 0 to 1
- start_block: float32 [4, 4, 8, 4, 3, 256], P('gx', 'gy', 'gz'), may hold values from -560 to 560
- neighbors: int32 [4, 4, 8, 6, 256], P('gx', 'gy', 'gz'), may hold values from 0 to 1151, as said below
- ghost_lists: int32 [8, 8, 16, 16], P('gx', 'gy', 'gz'), may hold values from 0 to 255
- embedding: float32 [2, 64], replicated, may hold values from 0.5 to 1.5
- radial_in: float32 [8, 128], replicated, may hold values from -2 to 2
- radial_out: float32 [128, 64], replicated, may hold values from -0.5 to 0.5
- readout: float32 [64], replicated, may hold values from -0.75 to 0.75
Outputs:
- next_block: float32 [4, 4, 8, 4, 3, 256], P('gx', 'gy', 'gz')
- diagonal_blocks: float32 [2, 4, 4], replicated
- offdiagonal_blocks: float32 [2, 4, 4], replicated
Inputs may be any that keep to these rules, and one draw needn't show every extreme that they name: `neighbors`: about two thirds of the slots name the device's own atoms, the rest ghost entries.
All inputs are finite; a program needn't handle non-finite values.
Results may differ from a plain program's by a relative error of at most 0.0003.
Values sent between devices are 32-bit elements; how exact they have to be, the bound alone decides.
A program may use at most 192 MiB of HBM per device.

v0:
```python
import jax
import jax.numpy as jnp
import numpy as np
from jax import lax
from jax.sharding import PartitionSpec as P

PRODUCTS = 2


SOFTEN = 0.25
CUTOFF = 4.0
HIGHEST = lax.Precision.HIGHEST


def with_halo(x, sides, width):
    for axis, dim in sides:
        size, length = (lax.axis_size(axis), x.shape[dim])
        up = [(i, (i + 1) % size) for i in range(size)]
        down = [(j, i) for i, j in up]
        last = lax.slice_in_dim(x, length - width, length, axis=dim)
        first = lax.slice_in_dim(x, 0, width, axis=dim)
        before = lax.ppermute(last, axis, up)
        after = lax.ppermute(first, axis, down)
        x = jnp.concatenate([before, x, after], axis=dim)
    return x


def from_behind(value, axis, steps):
    count = lax.axis_size(axis)
    pairs = [(source, (source + steps) % count) for source in range(count)]
    return lax.ppermute(value, axis, pairs)


def ghost_layout():
    chosen = []
    moves = []
    octants = []
    for number in range(64):
        coords = (number // 16, number // 4 % 4, number % 4)
        if all((member in (1, 2) for member in coords)):
            continue
        chosen.append(number)
        moves.append([int(member == 3) - int(member == 0) for member in coords])
        octants.append([(member + 1) % 2 for member in coords])
    return (np.array(chosen), np.array(moves), np.array(octants))


def block_energy(atom_table, embed_table, centers, neighbor, radial_in, radial_out, readout):
    fanout = neighbor.shape[0]
    width_block = neighbor.shape[1]
    flat_neighbor = neighbor.reshape(-1)
    center_coords = jnp.take(atom_table, centers, axis=1)
    neighbor_coords = jnp.take(atom_table, flat_neighbor, axis=1).reshape(3, fanout, width_block)
    displace = neighbor_coords - center_coords[:, None, :]
    distance = jnp.sqrt(jnp.sum(displace * displace, axis=0) + SOFTEN)
    direction = displace / distance[None]
    envelope = (1.0 - (distance / CUTOFF) ** 2) ** 2
    orders = jnp.arange(1, radial_in.shape[0] + 1).astype(jnp.float32)
    flat_distance = distance.reshape(-1)
    bessel = (
        jnp.sin(orders[:, None] * (jnp.pi / CUTOFF) * flat_distance[None, :])
        / flat_distance[None, :]
    )
    hidden = jax.nn.silu(jnp.dot(radial_in.T, bessel, precision=HIGHEST))
    radial = jnp.dot(radial_out.T, hidden, precision=HIGHEST).reshape(-1, fanout, width_block)
    pairing = jnp.take(embed_table, centers, axis=1)[:, None, :] * jnp.take(
        embed_table, flat_neighbor, axis=1
    ).reshape(-1, fanout, width_block)
    feature = radial * envelope[None] * pairing
    harmonic = jnp.concatenate([jnp.ones((1, fanout, width_block), jnp.float32), direction], axis=0)
    environ = jnp.einsum("ckb,mkb->cmb", feature, harmonic, precision=HIGHEST) / fanout
    project = jnp.einsum("cmb,mkb->ckb", environ, harmonic, precision=HIGHEST)
    mixed_feature = feature * project
    return jnp.sum(readout[:, None, None] * jax.nn.silu(mixed_feature))


def table_hessian(
    atom_table, embed_table, centers, neighbor, tangents, radial_in, radial_out, readout
):

    def energy(coords):
        return block_energy(coords, embed_table, centers, neighbor, radial_in, radial_out, readout)

    forces = jax.grad(energy)

    def apply_one(tangent):
        return jax.jvp(forces, (atom_table,), (tangent,))[1]

    return jax.vmap(apply_one)(tangents)


def on_device(
    positions,
    species,
    start_block,
    neighbors,
    ghost_lists,
    embedding,
    radial_in,
    radial_out,
    readout,
):
    chosen, moves, octants = ghost_layout()
    atoms_dev = positions.shape[-1]
    ghosts = ghost_lists.shape[-1]
    vectors = start_block.shape[3]
    devices = lax.axis_size("gx") * lax.axis_size("gy") * lax.axis_size("gz")
    scale_ip = 1.0 / (3.0 * atoms_dev * devices)
    octant_picks = ghost_lists.reshape(-1)
    own_coords = positions[0, 0, 0]
    own_species = species[0, 0, 0].astype(jnp.float32)
    packed = jnp.concatenate([own_coords, own_species[None]], axis=0)
    octant_atoms = jnp.take(packed, octant_picks, axis=1).reshape(4, 2, 2, 2, ghosts)
    beside_all = with_halo(octant_atoms, (("gx", 1), ("gy", 2), ("gz", 3)), 1)
    ghost_atoms = jnp.take(beside_all.reshape(4, 64, ghosts), chosen, axis=1)
    offsets = jnp.asarray(moves.T, jnp.float32)
    ghost_coords = ghost_atoms[:3] + offsets[:, :, None]
    atom_table = jnp.concatenate([own_coords, ghost_coords.reshape(3, -1)], axis=1)
    species_table = jnp.concatenate([own_species, ghost_atoms[3].reshape(-1)])
    kinds = jnp.arange(embedding.shape[0]).astype(jnp.float32)
    onehot = (species_table[None, :] == kinds[:, None]).astype(jnp.float32)
    embed_table = jnp.dot(embedding.T, onehot, precision=HIGHEST)
    table_width = atom_table.shape[1]
    neighbor_all = neighbors[0, 0, 0]
    block_size = min(256, atoms_dev)
    block_count = atoms_dev // block_size
    rows_tan = 3 * vectors

    def mean_gram(left_rows, right_rows):
        return jnp.dot(left_rows, right_rows.T, precision=HIGHEST) * scale_ip

    initial = start_block[0, 0, 0].reshape(vectors, 3 * atoms_dev)
    factor = jnp.linalg.cholesky(lax.psum(mean_gram(initial, initial), ("gx", "gy", "gz")))
    current = jax.scipy.linalg.solve_triangular(factor, initial, lower=True)
    previous = jnp.zeros_like(current)
    diagonals = []
    couplings = []
    for step_number in range(PRODUCTS):
        flat_block = current.reshape(rows_tan, atoms_dev)
        octant_tangent = jnp.take(flat_block, octant_picks, axis=1).reshape(
            rows_tan, 2, 2, 2, ghosts
        )
        around_tangent = with_halo(octant_tangent, (("gx", 1), ("gy", 2), ("gz", 3)), 1)
        ghost_tangent = jnp.take(
            around_tangent.reshape(rows_tan, 64, ghosts), chosen, axis=1
        ).reshape(rows_tan, -1)
        tangents = jnp.concatenate([flat_block, ghost_tangent], axis=1).reshape(
            vectors, 3, table_width
        )

        def add_block(running, block_number):
            centers = block_number * block_size + jnp.arange(block_size, dtype=jnp.int32)
            return (
                running
                + table_hessian(
                    atom_table,
                    embed_table,
                    centers,
                    neighbor_all,
                    tangents,
                    radial_in,
                    radial_out,
                    readout,
                ),
                None,
            )

        summed = lax.scan(
            add_block,
            jnp.zeros((vectors, 3, table_width), jnp.float32),
            jnp.arange(block_count, dtype=jnp.int32),
        )[0]
        summed = summed.reshape(rows_tan, table_width)
        local_portion = summed[:, :atoms_dev]
        ghost_part = summed[:, atoms_dev:].reshape(rows_tan, chosen.shape[0], ghosts)
        cells_full = jnp.zeros((rows_tan, 64, ghosts), jnp.float32).at[:, chosen].set(ghost_part)
        cells_full = cells_full.reshape(rows_tan, 4, 4, 4, ghosts)
        from_below = from_behind(cells_full[:, 3], "gx", 1)
        from_above = from_behind(cells_full[:, 0], "gx", -1)
        section_one = cells_full[:, 1:3] + jnp.stack([from_below, from_above], axis=1)
        from_below = from_behind(section_one[:, :, 3], "gy", 1)
        from_above = from_behind(section_one[:, :, 0], "gy", -1)
        section_two = section_one[:, :, 1:3] + jnp.stack([from_below, from_above], axis=2)
        from_below = from_behind(section_two[:, :, :, 3], "gz", 1)
        from_above = from_behind(section_two[:, :, :, 0], "gz", -1)
        octant_partial_sums = section_two[:, :, :, 1:3] + jnp.stack(
            [from_below, from_above], axis=3
        )
        flat_sums = octant_partial_sums.reshape(rows_tan, -1)
        local_portion = local_portion.at[:, octant_picks].add(flat_sums)
        product_block = local_portion.reshape(vectors, 3 * atoms_dev)
        proj_current, proj_previous = lax.psum(
            (mean_gram(current, product_block), mean_gram(previous, product_block)),
            ("gx", "gy", "gz"),
        )
        residue = (
            product_block
            - jnp.dot(proj_current.T, current, precision=HIGHEST)
            - jnp.dot(proj_previous.T, previous, precision=HIGHEST)
        )
        gram_matrix = lax.psum(mean_gram(residue, residue), ("gx", "gy", "gz"))
        factor = jnp.linalg.cholesky(gram_matrix)
        previous, current = (
            current,
            jax.scipy.linalg.solve_triangular(factor, residue, lower=True),
        )
        diagonals.append(proj_current)
        couplings.append(factor.T)
    return (
        current.reshape(1, 1, 1, vectors, 3, atoms_dev),
        jnp.stack(diagonals),
        jnp.stack(couplings),
    )


def solution(mesh):
    return jax.shard_map(
        on_device,
        mesh=mesh,
        in_specs=(
            P("gx", "gy", "gz", None, None),
            P("gx", "gy", "gz", None),
            P("gx", "gy", "gz", None, None, None),
            P("gx", "gy", "gz", None, None),
            P("gx", "gy", "gz", None),
            P(),
            P(),
            P(),
            P(),
        ),
        out_specs=(P("gx", "gy", "gz", None, None, None), P(), P()),
        check_vma=False,
    )
```

profile of v0, /device:TPU:1, one launch (start us, length us, event | category | flops | bytes accessed | tf_op | source)
XLA Modules:
  0.0 1433.0 jit_solution(3288755345176298491)
XLA Ops:
  9.4 66.6 %psum.49 = f32[4,4]{0,1:T(4,128)S(1)} all-reduce(f32[4,4]{0,1:T(4,128)S(1)} %fusion.108), channel_id=1, replica_groups=mesh['gx'=4,'gy'=4,'gz'=8] {'gx','gy','gz'}, use_global_device_ids=true, to_apply=%region_0.1 | all-reduce | flops 16 | bytes 128 | tf_op jit(solution)/shard_map/psum | solution.py:133
  139.5 5.2 multiply_reduce_fusion
  162.4 5.1 collective-permute-start.11
  190.5 6.7 gather_fusion.5
  216.0 9.8 fusion.106
  225.9 6.3 fusion.104
  232.3 5.2 fusion.102
  238.2 5.1 convolution_bitcast_fusion.3
  245.1 5.3 fusion.56
  253.3 5.8 copy.836
  260.2 7.4 fusion.65
  272.6 8.6 multiply_add_fusion.3
  281.2 56.5 %fusion.10 = f32[256,4,6,4]{2,3,1,0:T(4,128)} fusion(f32[4,64,6,256]{1,2,0,3:T(8,128)S(1)} %get-tuple-element.270, f32[256,4,64]{2,1,0:T(4,128)S(1)} %convolution_multiply_fusion.1), kind=kOutput, calls=%fused_computation.37 | convolution fusion | flops 18874368 | bytes 1933312 | tf_op jit(solution)/shard_map/while/body/eval_jaxpr/vmap(jvp(transpose(jvp(cmb,mkb->ckb))))/dot_general | solution.py:72
  337.7 4.9 fusion.64
  347.3 5.7 fusion.115
  353.0 56.9 %fusion.141 = f32[256,4,4,6]{3,1,2,0:T(4,128)} fusion(f32[256,4,64]{2,1,0:T(4,128)S(1)} %copy-done.48, f32[4,64,6,256]{1,2,0,3:T(8,128)S(1)} %copy-done.10, f32[64,6,256]{0,1,2:T(8,128)S(1)} %copy-done.19, f32[4,6,256]{1,0,2:T(4,128)S(1)} %copy-done.46, f32[64,6,256]{0,1,2:T(8,128)S(1)} %copy-done.7, f32[6,256]{0,1:T(8,128)S(1)} %copy.835), kind=kOutput, calls=%fused_computation.216 | convolution fusion | flops 20447232 | bytes 2750464 | tf_op jit(solution)/shard_map/while/body/eval_jaxpr/vmap(jvp(transpose(jvp(ckb,mkb->cmb))))/dot_general | solution.py:71
  409.8 15.5 %add_reduce_fusion.1 = (f32[4,6,256]{1,0,2:T(4,128)}, f32[4,64,6,256]{1,2,0,3:T(8,128)}) fusion(f32[4,64,6,256]{1,2,0,3:T(8,128)S(1)} %copy-done.10, f32[64,6,256]{0,1,2:T(8,128)S(1)} %copy-done.169, f32[64,6,256]{0,1,2:T(8,128)S(1)} %copy-done.7, f32[4,6,256]{1,0,2:T(4,128)S(1)} %copy-done.46, f32[6,256]{0,1:T(8,128)S(1)} %copy.835, ...), kind=kOutput, calls=%fused_computation.48 | convolution fusion | flops 31057920 | bytes 10615040 | tf_op jit(solution)/shard_map/while/body/eval_jaxpr/vmap(jvp(transpose(jvp(ckb,mkb->cmb))))/dot_general | solution.py:71
  425.3 4.8 copy.866
  432.9 7.6 convolution_bitcast_fusion.1
  453.5 9.0 fusion.168
  469.7 155.1 %scatter_fusion = f32[4,3,1152]{1,0,2:T(4,128)} fusion(f32[4,3,1152]{1,0,2:T(4,128)} %broadcast.878.clone.1, s32[1536]{0:T(1024)S(1)} %copy-done.110, f32[1536,4,3]{2,1,0:T(4,128)} %copy.875), kind=kCustom, calls=%fused_computation.16 | custom fusion | flops 18432 | bytes 227328 | tf_op jit(solution)/shard_map/while/body/eval_jaxpr/vmap(jvp(transpose(jvp(jit(_take)))))/scatter-add | solution.py:53
  626.3 26.4 %scatter_fusion.1 = f32[4,3,1152]{1,0,2:T(4,128)} fusion(f32[4,3,1152]{1,0,2:T(4,128)} %broadcast.878.clone.2, s32[256]{0:T(256)S(1)} %iota.87, f32[256,4,3]{2,1,0:T(4,128)} %copy.876), kind=kCustom, calls=%fused_computation.17 | custom fusion | flops 3072 | bytes 37888 | tf_op jit(solution)/shard_map/while/body/eval_jaxpr/vmap(jvp(transpose(jvp(jit(_take)))))/scatter-add | solution.py:52
  663.6 7.8 scatter_fusion.2
  672.4 4.8 collective-permute-start.12
  688.3 5.1 collective-permute-start.17
  700.0 68.0 %all-reduce.5 = (f32[4,4]{0,1:T(4,128)S(1)}, f32[4,4]{0,1:T(4,128)S(1)}) all-reduce(f32[4,4]{0,1:T(4,128)S(1)} %convolution_multiply_fusion.7, f32[4,4]{0,1:T(4,128)S(1)} %convolution_multiply_fusion.6), channel_id=1, replica_groups=mesh['gx'=4,'gy'=4,'gz'=8] {'gx','gy','gz'}, use_global_device_ids=true, to_apply=%region_18.31 | all-reduce | flops 32 | bytes 256 | tf_op jit(solution)/shard_map/psum | solution.py:192
  768.5 63.0 %psum.52 = f32[4,4]{0,1:T(4,128)S(1)} all-reduce(f32[4,4]{0,1:T(4,128)S(1)} %convolution_multiply_fusion.5), channel_id=1, replica_groups=mesh['gx'=4,'gy'=4,'gz'=8] {'gx','gy','gz'}, use_global_device_ids=true, to_apply=%region_20.33 | all-reduce | flops 16 | bytes 128 | tf_op jit(solution)/shard_map/psum | solution.py:201
  874.5 6.7 gather_fusion.12
  900.2 9.8 fusion.99
  910.1 6.3 fusion.97
  917.1 5.2 fusion.95
  922.4 5.1 convolution_bitcast_fusion.2
  929.3 5.3 fusion.59
  937.5 5.8 copy.907
  944.4 7.4 fusion.63
  951.9 4.8 fusion.119
  956.7 8.6 multiply_add_fusion.1
  965.4 56.5 %fusion.4 = f32[256,4,6,4]{2,3,1,0:T(4,128)} fusion(f32[4,64,6,256]{1,2,0,3:T(8,128)S(1)} %get-tuple-element.272, f32[256,4,64]{2,1,0:T(4,128)S(1)} %convolution_multiply_fusion.1), kind=kOutput, calls=%fused_computation.29 | convolution fusion | flops 18874368 | bytes 1933312 | tf_op jit(solution)/shard_map/while/body/eval_jaxpr/vmap(jvp(transpose(jvp(cmb,mkb->ckb))))/dot_general | solution.py:72
  1021.9 4.9 fusion.62
  1031.5 5.7 fusion.112
  1037.2 56.9 %fusion.138 = f32[256,4,4,6]{3,1,2,0:T(4,128)} fusion(f32[256,4,64]{2,1,0:T(4,128)S(1)} %copy-done.49, f32[4,64,6,256]{1,2,0,3:T(8,128)S(1)} %copy-done.9, f32[4,6,256]{1,0,2:T(4,128)S(1)} %copy-done.45, f32[64,6,256]{0,1,2:T(8,128)S(1)} %copy-done.20, f32[64,6,256]{0,1,2:T(8,128)S(1)} %copy-done.8, f32[6,256]{0,1:T(8,128)S(1)} %copy.835), kind=kOutput, calls=%fused_computation.213 | convolution fusion | flops 20447232 | bytes 2750464 | tf_op jit(solution)/shard_map/while/body/eval_jaxpr/vmap(jvp(transpose(jvp(ckb,mkb->cmb))))/dot_general | solution.py:71
  1094.0 15.5 %add_reduce_fusion = (f32[4,6,256]{1,0,2:T(4,128)}, f32[4,64,6,256]{1,2,0,3:T(8,128)}) fusion(f32[4,64,6,256]{1,2,0,3:T(8,128)S(1)} %copy-done.9, f32[64,6,256]{0,1,2:T(8,128)S(1)} %copy-done.170, f32[64,6,256]{0,1,2:T(8,128)S(1)} %copy-done.8, f32[4,6,256]{1,0,2:T(4,128)S(1)} %copy-done.45, f32[6,256]{0,1:T(8,128)S(1)} %copy.835, ...), kind=kOutput, calls=%fused_computation.44 | convolution fusion | flops 31057920 | bytes 10615040 | tf_op jit(solution)/shard_map/while/body/eval_jaxpr/vmap(jvp(transpose(jvp(ckb,mkb->cmb))))/dot_general | solution.py:71
  1115.2 7.8 convolution_bitcast_fusion
  1132.6 7.8 fusion.166
  1144.3 99.2 %scatter_fusion.4 = f32[4,3,1152]{1,0,2:T(4,128)S(1)} fusion(f32[4,3,1152]{1,0,2:T(4,128)S(1)} %broadcast.878.clone, s32[1536]{0:T(1024)S(1)} %copy-done.111, f32[1536,4,3]{2,1,0:T(4,128)} %copy.942), kind=kCustom, calls=%fused_computation.20 | custom fusion | flops 18432 | bytes 227328 | tf_op jit(solution)/shard_map/while/body/eval_jaxpr/vmap(jvp(transpose(jvp(jit(_take)))))/scatter-add | solution.py:53
  1245.0 25.0 %scatter_fusion.5 = f32[4,3,1152]{1,0,2:T(4,128)} fusion(f32[4,3,1152]{1,0,2:T(4,128)} %broadcast.878.clone.3, s32[256]{0:T(256)S(1)} %iota.89, f32[256,4,3]{2,1,0:T(4,128)S(1)} %copy.943), kind=kCustom, calls=%fused_computation.21 | custom fusion | flops 3072 | bytes 37888 | tf_op jit(solution)/shard_map/while/body/eval_jaxpr/vmap(jvp(transpose(jvp(jit(_take)))))/scatter-add | solution.py:52
  1297.6 67.5 %all-reduce.4 = (f32[4,4]{0,1:T(4,128)S(1)}, f32[4,4]{0,1:T(4,128)S(1)}) all-reduce(f32[4,4]{0,1:T(4,128)S(1)} %convolution_multiply_fusion.4, f32[4,4]{0,1:T(4,128)S(1)} %convolution_multiply_fusion.3), channel_id=1, replica_groups=mesh['gx'=4,'gy'=4,'gz'=8] {'gx','gy','gz'}, use_global_device_ids=true, to_apply=%region_36.49 | all-reduce | flops 32 | bytes 256 | tf_op jit(solution)/shard_map/psum | solution.py:192
  1365.8 63.0 %psum.55 = f32[4,4]{0,1:T(4,128)S(1)} all-reduce(f32[4,4]{0,1:T(4,128)S(1)} %convolution_multiply_fusion.2), channel_id=1, replica_groups=mesh['gx'=4,'gy'=4,'gz'=8] {'gx','gy','gz'}, use_global_device_ids=true, to_apply=%region_38.51 | all-reduce | flops 16 | bytes 128 | tf_op jit(solution)/shard_map/psum | solution.py:201
  (664 shorter events, 326.0 us)
Async XLA Ops:
  0.6 110.5 %copy-start = (f32[128,64]{0,1:T(8,128)S(1)}, f32[128,64]{0,1:T(8,128)}, u32[]{:S(2)}) copy-start(f32[128,64]{0,1:T(8,128)} %param.56) | copy-start | bytes 98308
  0.6 95.7 %copy-start.146 = (f32[3,56]{0,1:T(8,128)S(1)}, f32[3,56]{0,1:T(8,128)}, u32[]{:S(2)}) copy-start(f32[3,56]{0,1:T(8,128)} %constant.253.clone) | copy-start | bytes 2020
  0.7 99.7 %copy-start.168 = (f32[2,64]{1,0:T(2,128)S(1)}, f32[2,64]{1,0:T(2,128)}, u32[]{:S(2)}) copy-start(f32[2,64]{1,0:T(2,128)} %param.54) | copy-start | bytes 1540
  3.7 91.8 %copy-start.158 = (s32[128]{0:T(128)}, s32[128]{0:T(128)S(1)}, u32[]{:S(2)}) copy-start(s32[128]{0:T(128)S(1)} %fusion.254) | copy-start | bytes 1540
  4.5 78.4 %collective-permute-start = (f32[4,1,2,2,16]{4,1,3,2,0:T(1,128)S(1)}, f32[4,1,2,2,16]{4,1,3,2,0:T(1,128)S(1)}, u32[]{:S(2)}, u32[]{:S(2)}) collective-permute-start(f32[4,1,2,2,16]{4,1,3,2,0:T(1,128)S(1)} %get-tuple-element.240), channel_id=1, source_target_pairs={{0,32},{32,64},{64,96},{96,0},{1,33},{33,65},{65,97},{97,1},{2,34}... | collective-permute-start | bytes 3080 | tf_op jit(solution)/shard_map/ppermute | solution.py:22
  7.6 75.3 %collective-permute-start.1 = (f32[4,1,2,2,16]{4,1,3,2,0:T(1,128)S(1)}, f32[4,1,2,2,16]{4,1,3,2,0:T(1,128)S(1)}, u32[]{:S(2)}, u32[]{:S(2)}) collective-permute-start(f32[4,1,2,2,16]{4,1,3,2,0:T(1,128)S(1)} %get-tuple-element.241), channel_id=1, source_target_pairs={{32,0},{64,32},{96,64},{0,96},{33,1},{65,33},{97,65},{1,97},{34,2}... | collective-permute-start | bytes 3080 | tf_op jit(solution)/shard_map/ppermute | solution.py:23
  9.3 73.5 %copy-start.167 = (pred[128]{0:T(512)(128)(4,1)}, pred[128]{0:T(512)(128)(4,1)S(1)}, u32[]{:S(2)}) copy-start(pred[128]{0:T(512)(128)(4,1)S(1)} %compare_and_fusion.2) | copy-start | bytes 388
  80.0 12.1 collective-permute-start.6
  81.4 10.7 collective-permute-start.7
  83.0 3.9 collective-permute-start.2
  83.1 3.8 collective-permute-start.3
  86.9 8.5 collective-permute-start.4
  88.5 6.9 collective-permute-start.5
  92.1 68.7 %copy-start.71 = (f32[12,1,2,2,16]{0,4,3,2,1:T(8,128)}, f32[12,1,2,2,16]{0,4,3,2,1:T(8,128)S(1)}, u32[]{:S(2)}) copy-start(f32[12,1,2,2,16]{0,4,3,2,1:T(8,128)S(1)} %collective-permute-done.6) | copy-start | bytes 9220
  92.8 67.8 %collective-permute-start.8 = (f32[12,4,1,2,16]{0,4,3,2,1:T(8,128)}, f32[12,4,1,2,16]{0,4,3,2,1:T(8,128)}, u32[]{:S(2)}, u32[]{:S(2)}) collective-permute-start(f32[12,4,1,2,16]{0,4,3,2,1:T(8,128)} %get-tuple-element.223), channel_id=1, source_target_pairs={{0,8},{8,16},{16,24},{24,0},{1,9},{9,17},{17,25},{25,1},{2,10},{10... | collective-permute-start | bytes 18440 | tf_op jit(solution)/shard_map/ppermute | solution.py:22
  92.8 67.8 %collective-permute-start.9 = (f32[12,4,1,2,16]{0,4,3,2,1:T(8,128)}, f32[12,4,1,2,16]{0,4,3,2,1:T(8,128)}, u32[]{:S(2)}, u32[]{:S(2)}) collective-permute-start(f32[12,4,1,2,16]{0,4,3,2,1:T(8,128)} %get-tuple-element.224), channel_id=1, source_target_pairs={{8,0},{16,8},{24,16},{0,24},{9,1},{17,9},{25,17},{1,25},{10,2},{18... | collective-permute-start | bytes 18440 | tf_op jit(solution)/shard_map/ppermute | solution.py:23
  108.2 354.7 %copy-start.58 = (f32[6,256]{1,0:T(8,128)}, f32[6,256]{1,0:T(8,128)S(1)}, u32[]{:S(2)}) copy-start(f32[6,256]{1,0:T(8,128)S(1)} %sqrt.140) | copy-start | bytes 18436
  108.8 354.1 %copy-start.56 = (f32[6,256]{1,0:T(8,128)}, f32[6,256]{1,0:T(8,128)S(1)}, u32[]{:S(2)}) copy-start(f32[6,256]{1,0:T(8,128)S(1)} %get-tuple-element.259) | copy-start | bytes 18436
  162.4 12.6 collective-permute-start.10
  162.4 12.6 collective-permute-start.11
  168.2 294.6 %copy-start.100 = (f32[6,256]{1,0:T(8,128)}, f32[6,256]{1,0:T(8,128)S(1)}, u32[]{:S(2)}) copy-start(f32[6,256]{1,0:T(8,128)S(1)} %get-tuple-element.247) | copy-start | bytes 18436
  172.1 290.7 %copy-start.97 = (f32[6,256]{1,0:T(8,128)}, f32[6,256]{1,0:T(8,128)S(1)}, u32[]{:S(2)}) copy-start(f32[6,256]{1,0:T(8,128)S(1)} %div.343) | copy-start | bytes 18436
  281.2 56.5 %copy-start.29 = (f32[256,64,4,4]{1,3,2,0:T(4,128)S(1)}, f32[256,64,4,4]{1,3,2,0:T(4,128)}, u32[]{:S(2)}) copy-start(f32[256,64,4,4]{1,3,2,0:T(4,128)} %fusion.102) | copy-start | bytes 3145732
  353.0 56.9 %copy-start.4 = (f32[4,3,6,256]{2,1,0,3:T(4,128)S(1)}, f32[4,3,6,256]{2,1,0,3:T(4,128)}, u32[]{:S(2)}) copy-start(f32[4,3,6,256]{2,1,0,3:T(4,128)} %copy.1017) | copy-start | bytes 221188
  353.0 56.9 %copy-start.169 = (f32[64,6,256]{0,1,2:T(8,128)S(1)}, f32[64,6,256]{0,1,2:T(8,128)}, u32[]{:S(2)}) copy-start(f32[64,6,256]{0,1,2:T(8,128)} %get-tuple-element.267) | copy-start | bytes 1179652
  658.5 41.2 %copy-start.54 = (f32[4,768]{1,0:T(4,128)S(1)}, f32[4,768]{1,0:T(4,128)}, u32[]{:S(2)}) copy-start(f32[4,768]{1,0:T(4,128)} %copy-done.53) | copy-start | bytes 36868
  672.4 6.8 collective-permute-start.12
  677.2 4.4 collective-permute-start.13
  682.6 4.9 collective-permute-start.14
  682.7 4.9 collective-permute-start.15
  688.3 6.6 collective-permute-start.16
  688.3 6.6 collective-permute-start.17
  768.0 66.5 %copy-start.151 = (f32[4,4]{0,1:T(4,128)}, f32[4,4]{0,1:T(4,128)S(1)}, u32[]{:S(2)}) copy-start(f32[4,4]{0,1:T(4,128)S(1)} %get-tuple-element.154) | copy-start | bytes 196
  837.3 1.7 collective-permute-start.18
  838.0 3.3 collective-permute-start.19
  841.4 4.9 collective-permute-start.20
  841.6 4.7 collective-permute-start.21
  847.0 8.1 collective-permute-start.22
  849.2 9.9 collective-permute-start.23
  965.4 56.5 %copy-start.30 = (f32[256,64,4,4]{1,3,2,0:T(4,128)S(1)}, f32[256,64,4,4]{1,3,2,0:T(4,128)}, u32[]{:S(2)}) copy-start(f32[256,64,4,4]{1,3,2,0:T(4,128)} %fusion.95) | copy-start | bytes 3145732
  1037.2 56.9 %copy-start.2 = (f32[4,3,6,256]{2,1,0,3:T(4,128)S(1)}, f32[4,3,6,256]{2,1,0,3:T(4,128)}, u32[]{:S(2)}) copy-start(f32[4,3,6,256]{2,1,0,3:T(4,128)} %copy.1018) | copy-start | bytes 221188
  1037.2 56.9 %copy-start.170 = (f32[64,6,256]{0,1,2:T(8,128)S(1)}, f32[64,6,256]{0,1,2:T(8,128)}, u32[]{:S(2)}) copy-start(f32[64,6,256]{0,1,2:T(8,128)} %get-tuple-element.267) | copy-start | bytes 1179652
  1278.2 3.0 collective-permute-start.24
  1279.3 4.6 collective-permute-start.25
  1283.9 5.3 collective-permute-start.26
  1284.0 5.2 collective-permute-start.27
  1289.2 6.4 collective-permute-start.28
  1289.9 5.8 collective-permute-start.29
  (154 other events, 1574.9 us)
where the time goes:
time: 1460 us; the launch traced here: 1430 us
  matrix products  459 us (31%)
  other arithmetic  369 us (25%)
  blocking collectives  328 us (22%)
  local copies, waits for them, and re-layouts  195 us (13%)
  starting transfers between devices  50.4 us (3%)
  waiting for transfers between devices  27.1 us (2%)
    scatter-add x2, other arithmetic, block_energy(): jnp.take(atom_table, flat_neighbor, axis=1).reshape(3, fanout, width_block)  254 us
    dot_general x15, matrix products, block_energy(): jnp.einsum('ckb,mkb->cmb', feature, harmonic, precision=HIGHEST) / fanout  203 us
    dot_general x15, matrix products, block_energy(): project = jnp.einsum('cmb,mkb->ckb', environ, harmonic, precision=HIGHEST)  188 us
    psum x2, blocking collectives, on_device(): lax.psum((mean_gram(current, product_block), mean_gram(previous, product_...  136 us
    psum x2, blocking collectives, on_device(): gram_matrix = lax.psum(mean_gram(residue, residue), ('gx', 'gy', 'gz'))  126 us
    psum x1, blocking collectives, on_device(): lax.psum(mean_gram(initial, initial), ('gx', 'gy', 'gz'))  66.6 us
    scatter-add x2, other arithmetic, block_energy(): center_coords = jnp.take(atom_table, centers, axis=1)  51.4 us
    dot_general x6, matrix products, block_energy(): hidden = jax.nn.silu(jnp.dot(radial_in.T, bessel, precision=HIGHEST))  32.2 us
  transfers between devices with their start and end apart: 30, of which 14 were waited for; matrix products, arithmetic and copies ran while one was open for 6% of the time, Pallas kernels for 0%

commit v1 on v0

v1 whole, which is shorter than its diff:
```python
import functools
import math

import jax
import jax.numpy as jnp
import numpy as np
from jax import lax
from jax.experimental import pallas as pl
from jax.experimental.pallas import tpu as pltpu
from jax.sharding import PartitionSpec as P

AXES = ("gx", "gy", "gz")
SOFTEN = 0.25
CUTOFF = 4.0
F32 = jnp.float32
BF16 = jnp.bfloat16
ATOMS = 256
FAN = 6
CH = 64
HID = 128
NB = 8
COLS = 1152
ROWS = 16
HIGHEST = lax.Precision.HIGHEST
MESH = pl.DeviceIdType.MESH

SF, SF1, SF2, SP, SA, SB, SE = 0, 6, 12, 18, 24, 30, 36


def column_cells():
    lane = np.arange(128)
    octant = lane // 16
    own = np.stack([octant // 4 + 1, octant // 2 % 2 + 1, octant % 2 + 1])

    def shift(block, axis, by):
        block = block.copy()
        block[axis] += by
        return block

    def roll(block, by):
        return np.roll(block, by, axis=1)

    left, right = shift(own, 0, -2), shift(own, 0, 2)
    xs = roll(np.where(lane < 64, right, left), 64)
    bit = (lane // 32) % 2 == 1
    up = np.where(bit, own, roll(xs, -32))
    down = np.where(bit, roll(xs, 32), own)
    yb, ya = shift(up, 1, -2), shift(down, 1, 2)
    bit = (lane // 16) % 2 == 1
    pairs = ((own, xs), (yb, ya))
    up = [np.where(bit, a, roll(b, -16)) for a, b in pairs]
    down = [np.where(bit, roll(b, 16), a) for a, b in pairs]
    zb = [shift(m, 2, -2) for m in up]
    za = [shift(m, 2, 2) for m in down]
    return np.concatenate([xs, yb, ya] + zb + za, axis=1)


def table_constants():
    cells = column_cells()
    order = {}
    for number in range(64):
        m = (number // 16, number // 4 % 4, number % 4)
        if not all(x in (1, 2) for x in m):
            order[m] = len(order)
    rank = np.arange(cells.shape[1]) % 16
    ids = np.array([256 + order[tuple(int(x) for x in cells[:, n])] * 16 for n in range(cells.shape[1])]) + rank
    assert sorted(ids) == list(range(256, COLS))
    ids = np.concatenate([np.arange(256), ids]).astype(np.int32)
    moves = (cells == 3).astype(np.float32) - (cells == 0).astype(np.float32)
    offs = np.zeros((ROWS, COLS), np.float32)
    offs[12:15, 256:] = moves
    ones = np.zeros((32, 192), np.float32)
    for group in range(4):
        for k in range(FAN):
            ones[8 * group + k, (group * FAN + k) * 8 : (group * FAN + k) * 8 + 8] = 1.0
    return ids[:, None], offs, ones


def split3(x):
    high = x.astype(BF16)
    rest = x - high.astype(F32)
    mid = rest.astype(BF16)
    low = (rest - mid.astype(F32)).astype(BF16)
    return high, mid, low


def rows3(x):
    return jnp.concatenate(split3(x), axis=0)


def sum3(y):
    n = y.shape[0] // 3
    return (y[2 * n :] + y[n : 2 * n]) + y[:n]


def mm(a, b, contract=((1,), (0,))):
    return lax.dot_general(a, b, (contract, ((), ())), preferred_element_type=F32)


def mm_high(a, b):
    return jnp.dot(a, b, precision=HIGHEST, preferred_element_type=F32)


def sin_cos(x):
    q = jnp.floor(x * (2.0 / math.pi) + 0.5)
    y = x - q * 1.5703125
    y = y - q * 4.837512969970703125e-4
    y = y - q * 7.549789948768648e-8
    y2 = y * y
    s = y + y * y2 * (-1.6666654611e-1 + y2 * (8.3321608736e-3 - y2 * 1.9515295891e-4))
    c = 1.0 - 0.5 * y2 + y2 * y2 * (4.166664568298827e-2 + y2 * (-1.388731625493765e-3 + y2 * 2.443315711809948e-5))
    h = q - 4.0 * jnp.floor(q * 0.25)
    odd = (h == 1.0) | (h == 3.0)
    ss = jnp.where(odd, c, s)
    cc = jnp.where(odd, s, c)
    ss = jnp.where(h >= 2.0, -ss, ss)
    cc = jnp.where((h == 1.0) | (h == 2.0), -cc, cc)
    return ss, cc


def kernel(
    sizes, pos_ref, spc_ref, sb_ref, nbr_ref, gl_ref, emb_ref, rin_ref, rout_ref, rdo_ref, ids_ref, offs_ref, ones_ref,
    next_ref, diag_ref, off_ref,
    own, inc, tab, vtab, rtab, dt, grs, geo, sums, ub, bv, fs, acc, epv, wpad, rt2, embc, ghost, cb,
    sx, rx, sy, ry, sz, rz, arb, hsend, hrecv, asend, arecv,
):
    me = [lax.axis_index(a) for a in AXES]
    scale_ip = 1.0 / (3.0 * ATOMS * sizes[0] * sizes[1] * sizes[2])
    base = [0, sizes[0], sizes[0] + sizes[1]]

    def wrap(axis, by):
        return {AXES[axis]: lax.rem(me[axis] + by, sizes[axis])}

    barrier = pltpu.get_barrier_semaphore()
    for axis in range(3):
        for d in range(1, sizes[axis]):
            pl.semaphore_signal(barrier, inc=1, device_id=wrap(axis, d), device_id_type=MESH)

    lane = lax.broadcasted_iota(jnp.int32, (1, 128), 1)
    bit64 = (lane % 128) >= 64
    bit32 = (lane % 64) >= 32
    bit16 = (lane % 32) >= 16
    sub8 = lax.broadcasted_iota(jnp.int32, (8, 128), 0)
    lane8 = lax.broadcasted_iota(jnp.int32, (8, 128), 1)

    def roll(x, by):
        return pltpu.roll(x, by % 128, 1)

    pending = []

    def send(i, n, src, dst, axis, by):
        copy = pltpu.make_async_remote_copy(
            src_ref=src, dst_ref=dst, send_sem=hsend.at[i, n], recv_sem=hrecv.at[i, n],
            device_id=wrap(axis, by), device_id_type=MESH,
        )
        copy.start()
        pending.append(copy)
        return copy

    def ar_send(i, axis, tile):
        mine = base[axis] + me[axis]
        arb[i, mine] = tile
        for d in range(1, sizes[axis]):
            copy = pltpu.make_async_remote_copy(
                src_ref=arb.at[i, mine], dst_ref=arb.at[i, mine],
                send_sem=asend.at[i, base[axis] + d], recv_sem=arecv.at[i, mine],
                device_id=wrap(axis, d), device_id_type=MESH,
            )
            copy.start()
            pending.append(copy)

    def ar_recv(i, axis):
        for d in range(1, sizes[axis]):
            src = base[axis] + lax.rem(me[axis] + d, sizes[axis])
            pltpu.make_async_remote_copy(
                src_ref=arb.at[i, src], dst_ref=arb.at[i, src],
                send_sem=asend.at[i, base[axis] + d], recv_sem=arecv.at[i, src],
                device_id=wrap(axis, d), device_id_type=MESH,
            ).wait_recv()
        total = arb[i, base[axis]]
        for j in range(1, sizes[axis]):
            total = total + arb[i, base[axis] + j]
        return total

    def gram_rows(left, right):
        out = jnp.zeros((4, 128), F32)
        for w in range(4):
            prod = left[0:4, :] * right[w : w + 1, :]
            for c in (1, 2):
                prod = prod + left[4 * c : 4 * c + 4, :] * right[4 * c + w : 4 * c + w + 1, :]
            total = jnp.sum(prod, axis=1, keepdims=True) * scale_ip
            out = jnp.where(lane8[:4] == w, total, out)
        return out

    def entries(tile, row):
        out = [[None] * 4 for _ in range(4)]
        for w in range(4):
            col = jnp.broadcast_to(tile[:, w : w + 1], (8, 128))
            for u in range(4):
                out[u][w] = jnp.broadcast_to(col[row + u : row + u + 1, :], (8, 128))
        return out

    def place(vals):
        out = jnp.zeros((8, 128), F32)
        for n, val in enumerate(vals):
            if val is not None:
                out = jnp.where(sub8 == n, val, out)
        return out[0:4, 0:1]

    def matrix(get):
        out = jnp.zeros((8, 128), F32)
        for u in range(4):
            for w in range(4):
                val = get(u, w)
                if val is not None:
                    out = jnp.where((sub8 == u) & (lane8 == w), val, out)
        return out[0:4, 0:4]

    def cholesky(g):
        low = [[None] * 4 for _ in range(4)]
        inv_d = [None] * 4
        for j in range(4):
            total = g[j][j]
            for m in range(j):
                total = total - low[j][m] * low[j][m]
            low[j][j] = jnp.sqrt(total)
            inv_d[j] = 1.0 / low[j][j]
            for u in range(j + 1, 4):
                total = g[u][j]
                for m in range(j):
                    total = total - low[u][m] * low[j][m]
                low[u][j] = total * inv_d[j]
        inv = [[None] * 4 for _ in range(4)]
        for j in range(4):
            inv[j][j] = inv_d[j]
            for u in range(j + 1, 4):
                total = low[u][j] * inv[j][j]
                for m in range(j + 1, u):
                    total = total + low[u][m] * inv[m][j]
                inv[u][j] = -total * inv_d[u]
        return low, inv

    def columns_of(mat):
        return [place([mat[u][w] for u in range(4)]) for w in range(4)]

    def combine(cols, src, c):
        total = cols[0] * src[4 * c : 4 * c + 1, :]
        for w in range(1, 4):
            total = total + cols[w] * src[4 * c + w : 4 * c + w + 1, :]
        return total

    def fwd_x(i, block):
        sx[i] = block
        return (
            send(i, 0, sx.at[i], rx.at[i, 0], 0, 1),
            send(i, 1, sx.at[i], rx.at[i, 1], 0, sizes[0] - 1),
        )

    def fwd_x_done(i, copies):
        for copy in copies:
            copy.wait_recv()
        return roll(jnp.where(bit64, rx[i, 0], rx[i, 1]), 64)

    def fwd_y(i, block, xs):
        sy[i, 0] = jnp.where(bit32, block, roll(xs, -32))
        sy[i, 1] = jnp.where(bit32, roll(xs, 32), block)
        return (
            send(i, 2, sy.at[i, 0], ry.at[i, 0], 1, 1),
            send(i, 3, sy.at[i, 1], ry.at[i, 1], 1, sizes[1] - 1),
        )

    def fwd_y_done(i, copies):
        for copy in copies:
            copy.wait_recv()
        return ry[i, 0], ry[i, 1]

    def fwd_z(i, block, xs, yb, ya):
        for j, (a, b) in enumerate(((block, xs), (yb, ya))):
            sz[i, 0, :, 128 * j : 128 * j + 128] = jnp.where(bit16, a, roll(b, -16))
            sz[i, 1, :, 128 * j : 128 * j + 128] = jnp.where(bit16, roll(b, 16), a)
        return (
            send(i, 4, sz.at[i, 0], rz.at[i, 0], 2, 1),
            send(i, 5, sz.at[i, 1], rz.at[i, 1], 2, sizes[2] - 1),
        )

    def fwd_z_done(i, copies):
        for copy in copies:
            copy.wait_recv()
        return rz[i, 0], rz[i, 1]

    def give_back(i, con):
        sz[i, 0] = con[:, 640:896]
        sz[i, 1] = con[:, 896:1152]
        copies = (
            send(i, 4, sz.at[i, 0], rz.at[i, 1], 2, sizes[2] - 1),
            send(i, 5, sz.at[i, 1], rz.at[i, 0], 2, 1),
        )
        for copy in copies:
            copy.wait_recv()
        a_adj, b_adj = [], []
        for j in range(2):
            mu = rz[i, 1, :, 128 * j : 128 * j + 128]
            md = rz[i, 0, :, 128 * j : 128 * j + 128]
            a_adj.append(jnp.where(bit16, mu, md))
            b_adj.append(jnp.where(bit16, roll(mu, 16), roll(md, -16)))
        sy[i, 0] = con[:, 384:512] + a_adj[1]
        sy[i, 1] = con[:, 512:640] + b_adj[1]
        copies = (
            send(i, 2, sy.at[i, 0], ry.at[i, 1], 1, sizes[1] - 1),
            send(i, 3, sy.at[i, 1], ry.at[i, 0], 1, 1),
        )
        for copy in copies:
            copy.wait_recv()
        mu, md = ry[i, 1], ry[i, 0]
        mine = a_adj[0] + jnp.where(bit32, mu, md)
        sx[i] = con[:, 256:384] + b_adj[0] + jnp.where(bit32, roll(mu, 32), roll(md, -32))
        copies = (
            send(i, 0, sx.at[i], rx.at[i, 1], 0, sizes[0] - 1),
            send(i, 1, sx.at[i], rx.at[i, 0], 0, 1),
        )
        for copy in copies:
            copy.wait_recv()
        mine = mine + roll(jnp.where(bit64, rx[i, 0], rx[i, 1]), 64)
        return con[:, 0:256] + sum3(mm(rows3(mine), ghost[...], ((1,), (1,))))

    def pick(block):
        return sum3(mm(rows3(block), ghost[...]))

    for c in range(3):
        for v in range(4):
            own[4 * c + v : 4 * c + v + 1, :] = sb_ref[v, c : c + 1, :]
    own[12:15, :] = pos_ref[...]
    own[15:16, :] = spc_ref[...].astype(F32)
    atom_rows = lax.broadcasted_iota(jnp.int32, (ATOMS, 128), 0)
    ghost[...] = jnp.where(atom_rows == gl_ref[...], 1.0, 0.0).astype(BF16)
    block = pick(own[...])
    tile = jnp.concatenate([gram_rows(own, own), jnp.zeros((4, 128), F32)], axis=0)

    pl.semaphore_wait(barrier, sum(sizes) - 3)
    copies = fwd_x(0, block)
    ar_send(0, 0, tile)

    atom_lane = lax.broadcasted_iota(jnp.int32, (128, ATOMS), 1)

    def build(j, is_own):
        at = pl.ds(pl.multiple_of(j * 128, 128), 128)
        name = ids_ref[at, :]
        for k in range(FAN):
            part = jnp.where(nbr_ref[k : k + 1, :] == name, 1.0, 0.0)
            if is_own:
                part = part - jnp.where(atom_lane == name, 1.0, 0.0)
            inc[at, ATOMS * k : ATOMS * k + ATOMS] = part.astype(BF16)

    lax.fori_loop(0, 2, lambda j, z: (build(j, True), z)[1], 0)
    wpad[...] = jnp.zeros((2, 128, 128), F32)
    wpad[0, :, 0:CH] = rout_ref[...]
    wpad[1, 0:2, 0:CH] = emb_ref[...]
    wpad[1, 2:3, 0:CH] = rdo_ref[...]
    rt2[...] = wpad[0].T[0:CH, :]
    embc[...] = wpad[1].T[0:CH, :]
    wpad[1, 0:8, :] = rin_ref[...]
    wpad[1] = wpad[1].T

    xs = fwd_x_done(0, copies)
    copies = fwd_y(0, block, xs)
    ar_send(0, 1, ar_recv(0, 0))
    lax.fori_loop(2, 6, lambda j, z: (build(j, False), z)[1], 0)
    yb, ya = fwd_y_done(0, copies)
    copies = fwd_z(0, block, xs, yb, ya)
    ar_send(0, 2, ar_recv(0, 1))
    lax.fori_loop(6, 9, lambda j, z: (build(j, False), z)[1], 0)
    ga = jnp.where(own[15:16, :] < 0.5, embc[:, 0:1], embc[:, 1:2])
    epv[...] = ga
    zb, za = fwd_z_done(0, copies)

    tab[:, 0:256] = own[...]
    for at, part in ((256, xs), (384, yb), (512, ya), (640, zb), (896, za)):
        tab[:, at : at + part.shape[1]] = part + offs_ref[:, at : at + part.shape[1]]

    def gather(src):
        got = sum3(mm(rows3(src), inc[...]))
        for k in range(FAN):
            dt[:, k, :] = got[:, ATOMS * k : ATOMS * k + ATOMS]

    gather(tab[...])

    d3 = [dt[12 + h] for h in range(3)]
    dist2 = d3[0] * d3[0] + d3[1] * d3[1] + d3[2] * d3[2]
    dist = jnp.sqrt(dist2 + SOFTEN)
    inv_r = 1.0 / dist
    unit = [d * inv_r for d in d3]
    for h in range(3):
        geo[h] = unit[h]
    geo[3] = dist
    geo[4] = inv_r
    geo[5] = dt[15] + own[15:16, :]
    for h in range(3):
        for k in range(FAN):
            row = jnp.broadcast_to(unit[h][k : k + 1, :], (8, ATOMS))
            for l in range(2):
                ub[l, h * FAN + k] = row[:, 128 * l : 128 * l + 128]

    def tangents(product):
        for v in range(4):
            dv = [dt[4 * c + v] for c in range(3)]
            rp = geo[0] * dv[0] + geo[1] * dv[1] + geo[2] * dv[2]
            parts = [rp] + [(dv[h] - geo[h] * rp) * geo[4] for h in range(3)]
            for g in range(4):
                for k in range(FAN):
                    row = jnp.broadcast_to(parts[g][k : k + 1, :], (8, ATOMS))
                    for l in range(2):
                        bv[2 * v + l, g * FAN + k] = row[:, 128 * l : 128 * l + 128]

    tangents(0)

    order8 = (lax.broadcasted_iota(jnp.int32, (8, ATOMS), 0) + 1).astype(F32) * (math.pi / CUTOFF)

    def features(k, z):
        at = pl.ds(k, 1)
        r, ir, kind = geo[3, at, :], geo[4, at, :], geo[5, at, :]
        s, c = sin_cos(order8 * r)
        b0 = s * ir
        b1 = (order8 * c - b0) * ir
        b2 = -(order8 * order8) * b0 - 2.0 * b1 * ir
        rin_t = wpad[1, :, 0:8]
        z0, z1, z2 = (mm_high(rin_t, b) for b in (b0, b1, b2))
        sg = 1.0 / (1.0 + jnp.exp(-z0))
        sd = sg * (1.0 - sg)
        s1 = sg + z0 * sd
        s2 = sd * (2.0 + z0 * (1.0 - 2.0 * sg))
        h0 = z0 * sg
        h1 = s1 * z1
        h2 = s2 * z1 * z1 + s1 * z2
        r0, r1, r2 = (mm_high(rt2[...], h) for h in (h0, h1, h2))
        q = r * r * (1.0 / (CUTOFF * CUTOFF))
        sixth = FAN ** -0.5
        e0 = (1.0 - q) * (1.0 - q) * sixth
        e1 = (-4.0 / (CUTOFF * CUTOFF)) * r * (1.0 - q) * sixth
        e2 = (-4.0 / (CUTOFF * CUTOFF)) * (1.0 - 3.0 * q) * sixth
        w = epv[...] * jnp.where(kind < 0.5, embc[:, 0:1], embc[:, 1:2])
        f0 = r0 * e0 * w
        f1 = (r1 * e0 + r0 * e1) * w
        f2 = (r2 * e0 + 2.0 * r1 * e1 + r0 * e2) * w
        for slot, val in ((SF, f0), (SF1, f1), (SF2, f2)):
            for l in range(2):
                for t in range(8):
                    fs[8 * l + t, slot + k] = val[8 * t : 8 * t + 8, 128 * l : 128 * l + 128]
        return z

    lax.fori_loop(0, FAN, features, 0)

    ks = range(FAN)
    hs = range(3)

    def base_pass(i, z):
        l = i // 8
        t = lax.rem(i, 8)
        f = [fs[i, SF + k] for k in ks]
        f1 = [fs[i, SF1 + k] for k in ks]
        u = [[ub[l, h * FAN + k] for k in ks] for h in hs]
        rho = jnp.broadcast_to(embc[pl.ds(pl.multiple_of(t * 8, 8), 8), 2:3], (8, 128))
        e0 = sum(f[1:], f[0])
        e = [sum((f[k] * u[h][k] for k in ks[1:]), f[0] * u[h][0]) for h in hs]
        p, a, n = [], [], []
        for k in ks:
            pk = e0 + (e[0] * u[0][k] + e[1] * u[1][k] + e[2] * u[2][k])
            m = f[k] * pk
            sg = 1.0 / (1.0 + jnp.exp(-m))
            sd = sg * (1.0 - sg)
            ak = rho * (sg + m * sd)
            fs[i, SP + k] = pk
            fs[i, SA + k] = ak
            fs[i, SB + k] = rho * (sd * (2.0 + m * (1.0 - 2.0 * sg)))
            p.append(pk)
            a.append(ak)
            n.append(ak * f[k])
        for h in hs:
            fs[i, SE + h] = e[h]
        q0 = sum(n[1:], n[0])
        q = [sum((n[k] * u[h][k] for k in ks[1:]), n[0] * u[h][0]) for h in hs]
        for k in ks:
            fk = a[k] * p[k] + q0 + (q[0] * u[0][k] + q[1] * u[1][k] + q[2] * u[2][k])
            acc[l, k] += fk * f1[k]
            acc[2 + l, k] += fk * fs[i, SF2 + k]
            for h in hs:
                acc[l, FAN * (h + 1) + k] += n[k] * e[h] + f[k] * q[h]
                acc[2 + l, FAN * (h + 1) + k] += f1[k] * q[h]
        return z

    def clear():
        def zero(i, z):
            acc[i] = jnp.zeros((24, 8, 128), F32)
            return z
        lax.fori_loop(0, 8, zero, 0)

    ones = ones_ref[...].astype(BF16)

    def fold(v):
        out = []
        for l in range(2):
            hi, mid, lo = split3(acc[2 * v + l].reshape(192, 128))
            out.append((mm(ones, lo) + mm(ones, mid)) + mm(ones, hi))
        return jnp.concatenate(out, axis=1)

    clear()
    lax.fori_loop(0, 16, base_pass, 0)
    first, second = fold(0), fold(1)
    alpha, beta = first[0:8], second[0:8]
    force = [first[8 * h + 8 : 8 * h + 16] for h in hs]
    cross = [second[8 * h + 8 : 8 * h + 16] for h in hs]
    uv = unit[0] * force[0] + unit[1] * force[1] + unit[2] * force[2]
    sums[0] = alpha
    sums[1] = beta
    sums[2] = uv
    for h in hs:
        sums[3 + h] = force[h]
        sums[6 + h] = cross[h]

    def hvp(i, z):
        v = i // 16
        ch = lax.rem(i, 16)
        vl = 2 * v + ch // 8
        l = ch // 8
        f = [fs[ch, SF + k] for k in ks]
        rp = [bv[vl, k] for k in ks]
        u = lambda h, k: ub[l, h * FAN + k]
        du = lambda h, k: bv[vl, (h + 1) * FAN + k]
        df = [fs[ch, SF1 + k] * rp[k] for k in ks]
        de0 = sum(df[1:], df[0])
        de = []
        for h in hs:
            total = df[0] * u(h, 0) + f[0] * du(h, 0)
            for k in ks[1:]:
                total = total + (df[k] * u(h, k) + f[k] * du(h, k))
            de.append(total)
        e = [fs[ch, SE + h] for h in hs]
        dn, dfeat, n = [], [], []
        for k in ks:
            dp = de0
            for h in hs:
                dp = dp + (de[h] * u(h, k) + e[h] * du(h, k))
            pk, ak = fs[ch, SP + k], fs[ch, SA + k]
            da = fs[ch, SB + k] * (df[k] * pk + f[k] * dp)
            dn.append(da * f[k] + ak * df[k])
            n.append(ak * f[k])
            dfeat.append(da * pk + ak * dp)
        dq0 = sum(dn[1:], dn[0])
        dq = []
        for h in hs:
            total = dn[0] * u(h, 0) + n[0] * du(h, 0)
            for k in ks[1:]:
                total = total + (dn[k] * u(h, k) + n[k] * du(h, k))
            dq.append(total)
        for k in ks:
            tot = dfeat[k] + dq0 + (dq[0] * u(0, k) + dq[1] * u(1, k) + dq[2] * u(2, k))
            acc[vl, k] += fs[ch, SF1 + k] * tot
            for h in hs:
                acc[vl, FAN * (h + 1) + k] += (dn[k] * e[h] + n[k] * de[h]) + f[k] * dq[h]
        return z

    grs[12:16] = jnp.zeros((4, 8, ATOMS), F32)

    def finish_hvp():
        u3 = [geo[h] for h in hs]
        ir = geo[4]
        for v in range(4):
            got = fold(v)
            dv = [dt[4 * c + v] for c in range(3)]
            rp = u3[0] * dv[0] + u3[1] * dv[1] + u3[2] * dv[2]
            du = [(dv[h] - u3[h] * rp) * ir for h in hs]
            al, be, w0 = sums[0], sums[1], sums[2]
            fo = [sums[3 + h] for h in hs]
            cr = [sums[6 + h] for h in hs]
            dal = got[0:8] + be * rp + (cr[0] * du[0] + cr[1] * du[1] + cr[2] * du[2])
            dfo = [got[8 * h + 8 : 8 * h + 16] + rp * cr[h] for h in hs]
            duv = sum((du[h] * fo[h] + u3[h] * dfo[h] for h in hs[1:]), du[0] * fo[0] + u3[0] * dfo[0])
            back = rp * ir
            for h in hs:
                val = dal * u3[h] + al * du[h]
                val = val + ir * ((dfo[h] - du[h] * w0 - u3[h] * duv) - back * (fo[h] - u3[h] * w0))
                grs[4 * h + v] = val
        for k in ks:
            cb[:, ATOMS * k : ATOMS * k + ATOMS] = rows3(grs[:, k, :])
        return sum3(mm(cb[...], inc[...], ((1,), (1,))))

    clear()
    lax.fori_loop(0, 64, hvp, 0)
    low, inv = cholesky(entries(ar_recv(0, 2), 0))
    cols0 = columns_of(inv)
    for c in range(3):
        vtab[4 * c : 4 * c + 4, :] = combine(cols0, tab, c)
    image = give_back(1, finish_hvp())
    own[...] = image
    for c in range(3):
        rtab[4 * c : 4 * c + 4, 0:256] = combine(cols0, own, c)
    rtab[12:16, :] = jnp.zeros((4, COLS), F32)
    block = pick(rtab[:, 0:256])
    copies = fwd_x(2, block)
    tile = jnp.concatenate([gram_rows(vtab.at[:, 0:256], rtab.at[:, 0:256]), jnp.zeros((4, 128), F32)], axis=0)
    ar_send(1, 0, tile)
    xs = fwd_x_done(2, copies)
    copies = fwd_y(2, block, xs)
    ar_send(1, 1, ar_recv(1, 0))
    yb, ya = fwd_y_done(2, copies)
    copies = fwd_z(2, block, xs, yb, ya)
    ar_send(1, 2, ar_recv(1, 1))
    zb, za = fwd_z_done(2, copies)
    for at, part in ((256, xs), (384, yb), (512, ya), (640, zb), (896, za)):
        rtab[:, at : at + part.shape[1]] = part
    proj = entries(ar_recv(1, 2), 0)
    diag_ref[0] = matrix(lambda u, w: proj[u][w])
    cols = [place([proj[u][w] for w in range(4)]) for u in range(4)]
    for c in range(3):
        rtab[4 * c : 4 * c + 4, :] = rtab[4 * c : 4 * c + 4, :] - combine(cols, vtab, c)
    tile = jnp.concatenate([gram_rows(rtab.at[:, 0:256], rtab.at[:, 0:256]), jnp.zeros((4, 128), F32)], axis=0)
    ar_send(2, 0, tile)

    gather(rtab[...])
    tangents(1)
    clear()
    lax.fori_loop(0, 16, hvp, 0)
    ar_send(2, 1, ar_recv(2, 0))
    lax.fori_loop(16, 32, hvp, 0)
    ar_send(2, 2, ar_recv(2, 1))
    lax.fori_loop(32, 64, hvp, 0)
    low, inv = cholesky(entries(ar_recv(2, 2), 0))
    off_ref[0] = matrix(lambda u, w: low[w][u] if w >= u else None)
    cols1 = columns_of(inv)
    own[...] = give_back(3, finish_hvp())
    for c in range(3):
        tab[4 * c : 4 * c + 4, 0:256] = combine(cols1, rtab.at[:, 0:256], c)
    for c in range(3):
        rtab[4 * c : 4 * c + 4, 0:256] = combine(cols1, own, c)
    image = rtab.at[:, 0:256]
    tile = jnp.concatenate([gram_rows(tab.at[:, 0:256], image), gram_rows(vtab.at[:, 0:256], image)], axis=0)
    for axis in range(3):
        ar_send(3, axis, tile)
        tile = ar_recv(3, axis)
    proj = entries(tile, 0)
    prev = entries(tile, 4)
    cols = [place([proj[u][w] for w in range(4)]) for u in range(4)]
    cols_p = [place([prev[u][w] for w in range(4)]) for u in range(4)]
    for c in range(3):
        own[4 * c : 4 * c + 4, :] = (
            rtab[4 * c : 4 * c + 4, 0:256]
            - combine(cols, tab.at[:, 0:256], c)
            - combine(cols_p, vtab.at[:, 0:256], c)
        )
    tile = jnp.concatenate([gram_rows(own, own), jnp.zeros((4, 128), F32)], axis=0)
    ar_send(4, 0, tile)
    diag_ref[1] = matrix(lambda u, w: proj[u][w])
    tile = ar_recv(4, 0)
    for axis in (1, 2):
        ar_send(4, axis, tile)
        tile = ar_recv(4, axis)
    low, inv = cholesky(entries(tile, 0))
    cols = columns_of(inv)
    for c in range(3):
        last = combine(cols, own, c)
        for v in range(4):
            next_ref[v, c : c + 1, :] = last[v : v + 1, :]
    off_ref[1] = matrix(lambda u, w: low[w][u] if w >= u else None)
    for copy in pending:
        copy.wait_send()


def solution(mesh):
    sizes = tuple(mesh.shape[a] for a in AXES)
    ids, offs, ones = table_constants()
    total = sum(sizes)

    def on_device(positions, species, start_block, neighbors, ghost_lists, embedding, radial_in, radial_out, readout):
        vmem = pl.BlockSpec(memory_space=pltpu.VMEM)
        vm = lambda *shape: pltpu.VMEM(shape, F32)
        out = pl.pallas_call(
            functools.partial(kernel, sizes),
            out_shape=(
                jax.ShapeDtypeStruct((4, 3, ATOMS), F32),
                jax.ShapeDtypeStruct((2, 4, 4), F32),
                jax.ShapeDtypeStruct((2, 4, 4), F32),
            ),
            in_specs=[vmem] * 12,
            out_specs=(vmem, vmem, vmem),
            scratch_shapes=[
                vm(ROWS, ATOMS),
                pltpu.VMEM((COLS, FAN * ATOMS), BF16),
                vm(ROWS, COLS), vm(ROWS, COLS), vm(ROWS, COLS),
                vm(ROWS, 8, ATOMS), vm(ROWS, 8, ATOMS),
                vm(6, 8, ATOMS), vm(9, 8, ATOMS),
                vm(2, 18, 8, 128), vm(8, 24, 8, 128),
                vm(16, 39, 8, 128), vm(8, 24, 8, 128),
                vm(CH, ATOMS), vm(2, 128, 128), vm(CH, 128), vm(CH, 128),
                pltpu.VMEM((ATOMS, 128), BF16),
                pltpu.VMEM((3 * ROWS, FAN * ATOMS), BF16),
                vm(4, ROWS, 128), vm(4, 2, ROWS, 128),
                vm(4, 2, ROWS, 128), vm(4, 2, ROWS, 128),
                vm(4, 2, ROWS, 256), vm(4, 2, ROWS, 256),
                vm(5, total, 8, 128),
                pltpu.SemaphoreType.DMA((4, 6)), pltpu.SemaphoreType.DMA((4, 6)),
                pltpu.SemaphoreType.DMA((5, total)), pltpu.SemaphoreType.DMA((5, total)),
            ],
            compiler_params=pltpu.CompilerParams(
                collective_id=0, has_side_effects=True, vmem_limit_bytes=48 * 1024 * 1024
            ),
        )(
            positions[0, 0, 0], species[0, 0, 0][None], start_block[0, 0, 0], neighbors[0, 0, 0],
            ghost_lists.reshape(1, 128), embedding, radial_in, radial_out, readout[None],
            jnp.asarray(ids), jnp.asarray(offs), jnp.asarray(ones),
        )
        return out[0][None, None, None], out[1], out[2]

    return jax.shard_map(
        on_device,
        mesh=mesh,
        in_specs=(
            P("gx", "gy", "gz", None, None),
            P("gx", "gy", "gz", None),
            P("gx", "gy", "gz", None, None, None),
            P("gx", "gy", "gz", None, None),
            P("gx", "gy", "gz", None),
            P(), P(), P(), P(),
        ),
        out_specs=(P("gx", "gy", "gz", None, None, None), P(), P()),
        check_vma=False,
    )
```

time: 1460 us -> 106 us (0.07); the launches traced: 1430 us -> 105 us
  matrix products: 459 us -> 0 us
  other arithmetic: 369 us -> 0 us
  blocking collectives: 328 us -> 0 us
  local copies, waits for them, and re-layouts: 195 us -> 6.47 us
  Pallas kernels: 0 us -> 97.8 us
  starting transfers between devices: 50.4 us -> 0 us
  waiting for transfers between devices: 27.1 us -> 0 us
    dot_general x54 -> x0, matrix products: 457 us -> none  [the longest x15 203 us: block_energy(): jnp.einsum('ckb,mkb->cmb', feature, harmonic, precision=HIGHEST) / fanout]
    psum x5 -> x0, blocking collectives: 328 us -> none  [the longest x2 136 us: on_device(): lax.psum((mean_gram(current, product_block), mean_gram(previous, product_...]
    scatter-add x6 -> x0, other arithmetic: 309 us -> none  [the longest x2 254 us: block_energy(): jnp.take(atom_table, flat_neighbor, axis=1).reshape(3, fanout, width_block)]
    pallas_call x0 -> x1, Pallas kernels: none -> 97.8 us  [on_device(): pl.pallas_call(functools.partial(kernel, sizes), out_shape=(jax.ShapeDtyp...]
    ppermute x30 -> x0, starting transfers between devices: 50.4 us -> none  [the longest x12 21.6 us: from_behind(): return lax.ppermute(value, axis, pairs)]
    gather x17 -> x0, local copies, waits for them, and re-layouts: 45 us -> none  [the longest x5 23.4 us: block_energy(): jnp.take(atom_table, flat_neighbor, axis=1).reshape(3, fanout, width_block)]
    reshape x24 -> x1, local copies, waits for them, and re-layouts: 35 us -> 0.78 us  [on_device(): ghost_lists.reshape(1, 128)]
    ppermute x30 -> x0, waiting for transfers between devices: 27.1 us -> none  [the longest x12 16.1 us: from_behind(): return lax.ppermute(value, axis, pairs)]
  transfers between devices with their start and end apart: 30 -> 0, of which waited for: 14 -> 0; matrix products, arithmetic and copies ran while one was open for 6% -> 0% of each run, Pallas kernels for 0% -> 0%
where the time goes in v1:
time: 106 us; the launch traced here: 105 us
  Pallas kernels  97.8 us (92%)
  local copies, waits for them, and re-layouts  6.47 us (6%)
    pallas_call x1, Pallas kernels, on_device(): pl.pallas_call(functools.partial(kernel, sizes), out_shape=(jax.ShapeDtyp...  97.8 us
    unnamed x23, local copies, waits for them, and re-layouts  5.7 us

profile of v1, /device:TPU:1, one launch (start us, length us, event | category | flops | bytes accessed | tf_op | source)
XLA Modules:
  0.0 104.9 jit_solution(9805780871523905860)
XLA Ops:
  0.6 0.0 copy-start.7
  0.6 0.8 reshape.9.gl_ref
  1.4 0.7 copy.25
  2.1 0.0 copy-start.1
  2.1 0.7 copy.24
  2.8 0.7 copy.23
  3.5 0.0 copy-done.7
  3.5 0.0 copy-start.2
  3.6 0.0 copy-start.3
  3.6 0.0 copy-start.4
  3.6 0.0 copy-start.5
  3.6 0.0 copy-start.6
  3.6 0.1 copy.16.rout_ref
  3.7 0.0 copy-done.1
  3.7 0.6 copy-done.2
  4.3 0.0 copy-done.3
  4.3 0.0 copy-done.4
  4.3 0.0 copy-done.5
  4.3 0.0 copy-done.6
  4.3 0.0 copy-start
  4.3 1.1 %copy-done = s32[1152,1]{1,0:T(8,128)S(1)} copy-done((s32[1152,1]{1,0:T(8,128)S(1)}, s32[1152,1]{1,0:T(8,128)}, u32[]{:S(2)}) %copy-start) | copy-done | bytes 4632
  5.4 97.8 %shard_map.139 = (f32[4,3,256]{2,1,0:T(4,128)S(1)}, f32[2,4,4]{2,1,0:T(4,128)S(1)}, f32[2,4,4]{2,1,0:T(4,128)S(1)}) custom-call(f32[3,256]{1,0:T(4,128)S(1)} %bitcast.14, s32[1,256]{1,0:T(1,128)S(1)} %bitcast.16, f32[4,3,256]{2,1,0:T(4,128)S(1)} %bitcast.12, s32[6,256]{1,0:T(8,128)S(1)} %bitcast.13, s32[1,128]{1,0:T(1,128)S(1)} %reshape.9.gl_ref, ...), custom_call_target="tpu_custom_call" | custom-call | tf_op jit(solution)/shard_map/pallas_call | solution.py:675
  103.2 0.6 copy.17
  103.8 0.6 copy.28
  104.4 0.6 copy.29
Async XLA Ops:
  0.6 2.9 %copy-start.7 = (f32[128,64]{0,1:T(8,128)S(1)}, f32[128,64]{0,1:T(8,128)}, u32[]{:S(2)}) copy-start(f32[128,64]{0,1:T(8,128)} %param.19) | copy-start | bytes 98308
  2.1 1.6 %copy-start.1 = (f32[16,1152]{1,0:T(8,128)S(1)}, f32[16,1152]{1,0:T(8,128)}, u32[]{:S(2)}) copy-start(f32[16,1152]{1,0:T(8,128)} %constant.7.clone.offs_ref) | copy-start | bytes 221188
  3.5 0.8 copy-start.2
  3.6 0.8 copy-start.3
  3.6 0.7 copy-start.4
  3.6 0.7 copy-start.5
  3.6 0.7 copy-start.6
  4.3 1.1 %copy-start = (s32[1152,1]{1,0:T(8,128)S(1)}, s32[1152,1]{1,0:T(8,128)}, u32[]{:S(2)}) copy-start(s32[1152,1]{1,0:T(8,128)} %constant.6.clone.ids_ref) | copy-start | bytes 13828

commit v2 on v1

v2 whole, which is shorter than its diff:
```python
import functools
import itertools
import math

import jax
import jax.numpy as jnp
import numpy as np
from jax import lax
from jax.experimental import pallas as pl
from jax.experimental.pallas import tpu as pltpu
from jax.sharding import PartitionSpec as P

AXES = ("gx", "gy", "gz")
SOFTEN = 0.25
CUTOFF = 4.0
F32 = jnp.float32
BF16 = jnp.bfloat16
ATOMS = 256
FAN = 6
CH = 64
HID = 128
NB = 8
COLS = 1152
ROWS = 16
HIGHEST = lax.Precision.HIGHEST
MESH = pl.DeviceIdType.MESH

SF, SF1, SF2, SP, SA, SB, SE = 0, 6, 12, 18, 24, 30, 36


def neighbour_cells():
    shifts = [s for s in itertools.product((-1, 0, 1), repeat=3) if any(s)]
    shifts.sort(key=lambda s: sum(map(abs, s)))
    out, first = [], 0
    for s in shifts:
        octants = list(itertools.product(*[{1: (0,), -1: (1,), 0: (0, 1)}[x] for x in s]))
        out.append((s, first, octants))
        first += len(octants)
    return out


CELLS = neighbour_cells()
GHOST = 56


def constants():
    order = {}
    for number in range(64):
        m = (number // 16, number // 4 % 4, number % 4)
        if not all(x in (1, 2) for x in m):
            order[m] = len(order)
    out = np.zeros((32, 128), np.float32)
    ids = list(range(256))
    moves = []
    octant_of = []
    for s, _, octants in CELLS:
        for o in octants:
            m = tuple(2 * x + y + 1 for x, y in zip(s, o))
            ids += [256 + 16 * order[m] + r for r in range(16)]
            moves += [s] * 16
            octant_of.append(4 * o[0] + 2 * o[1] + o[2])
    assert sorted(ids) == list(range(COLS))
    out[0:9] = np.array(ids).reshape(9, 128)
    out[9] = -1.0
    out[9, :GHOST] = octant_of
    out[10:31] = np.array(moves).T.reshape(21, 128)
    return out


def split3(x):
    high = x.astype(BF16)
    rest = x - high.astype(F32)
    mid = rest.astype(BF16)
    low = (rest - mid.astype(F32)).astype(BF16)
    return high, mid, low


def rows3(x):
    return jnp.concatenate(split3(x), axis=0)


def sum3(y):
    n = y.shape[0] // 3
    return (y[2 * n :] + y[n : 2 * n]) + y[:n]


def mm(a, b, contract=((1,), (0,))):
    return lax.dot_general(a, b, (contract, ((), ())), preferred_element_type=F32)


def mm_high(a, b):
    return jnp.dot(a, b, precision=HIGHEST, preferred_element_type=F32)


def sin_cos(x):
    q = jnp.floor(x * (2.0 / math.pi) + 0.5)
    y = x - q * 1.5703125
    y = y - q * 4.837512969970703125e-4
    y = y - q * 7.549789948768648e-8
    y2 = y * y
    s = y + y * y2 * (-1.6666654611e-1 + y2 * (8.3321608736e-3 - y2 * 1.9515295891e-4))
    c = 1.0 - 0.5 * y2 + y2 * y2 * (4.166664568298827e-2 + y2 * (-1.388731625493765e-3 + y2 * 2.443315711809948e-5))
    h = q - 4.0 * jnp.floor(q * 0.25)
    odd = (h == 1.0) | (h == 3.0)
    ss = jnp.where(odd, c, s)
    cc = jnp.where(odd, s, c)
    ss = jnp.where(h >= 2.0, -ss, ss)
    cc = jnp.where((h == 1.0) | (h == 2.0), -cc, cc)
    return ss, cc


def kernel(
    sizes, pos_ref, spc_ref, sb_ref, nbr_ref, gl_ref, emb_ref, rin_ref, rout_ref, rdo_ref, cst_ref,
    next_ref, diag_ref, off_ref,
    own, inc, tab, v1, w1, r1, v2, dt, grs, geo, sums, ub, bv, fs, acc, epv, wpad, w2, embc, ghost, glw, cb,
    hs_buf, hr_buf, arb, hsend, hrecv, asend, arecv,
):
    gx, gy, gz = (lax.axis_index(a) for a in AXES)
    scale_ip = 1.0 / (3.0 * ATOMS * sizes[0] * sizes[1] * sizes[2])

    def beside(s):
        return {
            a: lax.rem(i + (x + n), n) for a, i, x, n in zip(AXES, (gx, gy, gz), s, sizes) if x
        }

    nx, ny, nz = sizes[0] // 2, sizes[1], sizes[2] // 2
    groups = (
        [o for o in itertools.product(range(nx), range(2), (0,), (0,), range(2)) if any(o)],
        [o for o in itertools.product((0,), (0,), range(ny), range(nz), (0,)) if any(o)],
    )
    starts = (0, len(groups[0]) + 1)

    def partner(o):
        a = lax.rem(gx // 2 + o[0], nx)
        b = lax.rem(lax.rem(gx, 2) + o[1], 2)
        c = lax.rem(gy + o[2], ny)
        d = lax.rem(gz // 2 + o[3], nz)
        e = lax.rem(lax.rem(gz, 2) + o[4], 2)
        return {"gx": 2 * a + b, "gy": c, "gz": 2 * d + e}, (4 * a + 2 * b + e, nz * c + d)

    barrier = pltpu.get_barrier_semaphore()
    for s, _, _ in CELLS:
        pl.semaphore_signal(barrier, inc=1, device_id=beside(s), device_id_type=MESH)
    for group in groups:
        for o in group:
            pl.semaphore_signal(barrier, inc=1, device_id=partner(o)[0], device_id_type=MESH)

    lane8 = lax.broadcasted_iota(jnp.int32, (8, 128), 1)
    sub8 = lax.broadcasted_iota(jnp.int32, (8, 128), 0)

    pending = []

    def ar_send(i, g, tile):
        mine = starts[g] + partner((0,) * 5)[1][g]
        arb[i, mine] = tile
        for n, o in enumerate(groups[g]):
            copy = pltpu.make_async_remote_copy(
                src_ref=arb.at[i, mine], dst_ref=arb.at[i, mine],
                send_sem=asend.at[i, starts[g] + n], recv_sem=arecv.at[i, mine],
                device_id=partner(o)[0], device_id_type=MESH,
            )
            copy.start()
            pending.append(copy)

    def ar_recv(i, g):
        for n, o in enumerate(groups[g]):
            device, at = partner(o)
            src = starts[g] + at[g]
            pltpu.make_async_remote_copy(
                src_ref=arb.at[i, src], dst_ref=arb.at[i, src],
                send_sem=asend.at[i, starts[g] + n], recv_sem=arecv.at[i, src],
                device_id=device, device_id_type=MESH,
            ).wait_recv()
        parts = [arb[i, starts[g] + j] for j in range(len(groups[g]) + 1)]
        while len(parts) > 1:
            parts = [a + b for a, b in zip(parts[::2], parts[1::2])] + parts[len(parts) // 2 * 2 :]
        return parts[0]

    def halo_send(i, sign):
        copies = []
        for n, (s, first, octants) in enumerate(CELLS):
            at = pl.ds(first, len(octants))
            copy = pltpu.make_async_remote_copy(
                src_ref=hs_buf.at[i, at], dst_ref=hr_buf.at[i, at],
                send_sem=hsend.at[i, n], recv_sem=hrecv.at[i, n],
                device_id=beside(tuple(sign * x for x in s)), device_id_type=MESH,
            )
            copy.start()
            copies.append(copy)
        pending.extend(copies)
        return copies

    def halo_wait(copies):
        for copy in copies:
            copy.wait_recv()

    def turn(x):
        for b in (2, 1, 0):
            by = 1 << b
            sbit = (sub8 & by) != 0
            lbit = (lane8 & (16 * by)) != 0
            low = pltpu.roll(pltpu.roll(x, by, 0), 128 - 16 * by, 1)
            high = low if b == 2 else pltpu.roll(pltpu.roll(x, 8 - by, 0), 16 * by, 1)
            x = jnp.where(sbit == lbit, x, jnp.where(sbit, low, high))
        return x

    def pack(i, src):
        got = sum3(mm(rows3(src), ghost[...]))
        flat = jnp.concatenate([turn(got[0:8]), turn(got[8:16])], axis=1)
        hs_buf[i] = mm(spread, rows3(flat))

    def unpack(i, dst, shifted):
        for j in range(7):
            at = pl.ds(256 + 128 * j, 128)
            for t in range(2):
                part = turn(hr_buf[i, 8 * j : 8 * j + 8, 128 * t : 128 * t + 128])
                if t == 1 and shifted:
                    rows = [jnp.zeros((4, 128), F32)] + [cst_ref[10 + 7 * h + j : 11 + 7 * h + j, :] for h in range(3)]
                    part = part + jnp.concatenate(rows + [jnp.zeros((1, 128), F32)], axis=0)
                dst[8 * t : 8 * t + 8, at] = part

    def pack_back(i, con):
        for j in range(7):
            for t in range(2):
                part = con[8 * t : 8 * t + 8, 128 * j : 128 * j + 128]
                hs_buf[i, 8 * j : 8 * j + 8, 128 * t : 128 * t + 128] = turn(part)

    def unpack_back(i):
        hi, mid, lo = split3(hr_buf[i])
        flat = (mm(collect, lo) + mm(collect, mid)) + mm(collect, hi)
        both = jnp.concatenate([turn(flat[:, 0:128]), turn(flat[:, 128:256])], axis=0)
        return sum3(mm(rows3(both), ghost[...], ((1,), (1,))))

    def gram_rows(left, right):
        out = jnp.zeros((4, 128), F32)
        for w in range(4):
            prod = left[0:4, :] * right[w : w + 1, :]
            for c in (1, 2):
                prod = prod + left[4 * c : 4 * c + 4, :] * right[4 * c + w : 4 * c + w + 1, :]
            total = jnp.sum(prod, axis=1, keepdims=True) * scale_ip
            out = jnp.where(lane8[:4] == w, total, out)
        return out

    def entries(tile, row):
        out = [[None] * 4 for _ in range(4)]
        for w in range(4):
            col = jnp.broadcast_to(tile[:, w : w + 1], (8, 128))
            for u in range(4):
                out[u][w] = jnp.broadcast_to(col[row + u : row + u + 1, :], (8, 128))
        return out

    def place(vals):
        out = jnp.zeros((8, 128), F32)
        for n, val in enumerate(vals):
            if val is not None:
                out = jnp.where(sub8 == n, val, out)
        return out[0:4, 0:1]

    def matrix(get):
        out = jnp.zeros((8, 128), F32)
        for u in range(4):
            for w in range(4):
                val = get(u, w)
                if val is not None:
                    out = jnp.where((sub8 == u) & (lane8 == w), val, out)
        return out[0:4, 0:4]

    def cholesky(g):
        low = [[None] * 4 for _ in range(4)]
        inv_d = [None] * 4
        for j in range(4):
            total = g[j][j]
            for m in range(j):
                total = total - low[j][m] * low[j][m]
            low[j][j] = jnp.sqrt(total)
            inv_d[j] = 1.0 / low[j][j]
            for u in range(j + 1, 4):
                total = g[u][j]
                for m in range(j):
                    total = total - low[u][m] * low[j][m]
                low[u][j] = total * inv_d[j]
        inv = [[None] * 4 for _ in range(4)]
        for j in range(4):
            inv[j][j] = inv_d[j]
            for u in range(j + 1, 4):
                total = low[u][j] * inv[j][j]
                for m in range(j + 1, u):
                    total = total + low[u][m] * inv[m][j]
                inv[u][j] = -total * inv_d[u]
        return low, inv

    def columns_of(mat):
        return [place([mat[u][w] for u in range(4)]) for w in range(4)]

    def combine(cols, src, c):
        total = cols[0] * src[4 * c : 4 * c + 1, :]
        for w in range(1, 4):
            total = total + cols[w] * src[4 * c + w : 4 * c + w + 1, :]
        return total

    for c in range(3):
        own[4 * c : 4 * c + 4, :] = sb_ref[c]
        own[12 + c : 13 + c, :] = pos_ref[c]
    own[15:16, :] = spc_ref[...].astype(F32)
    glw[...] = jnp.zeros((8, 128), jnp.int32)
    for n in range(8):
        glw[n : n + 1, 0:16] = gl_ref[n // 4, n // 2 % 2, n % 2 : n % 2 + 1, :]
    names = glw[0:1, :]
    for n in range(1, 8):
        names = names + pltpu.roll(glw[n : n + 1, :], 16 * n, 1)
    atom_rows = lax.broadcasted_iota(jnp.int32, (ATOMS, 128), 0)
    ghost[...] = jnp.where(atom_rows == names, 1.0, 0.0).astype(BF16)
    wpad[1] = jnp.zeros((128, 128), F32)
    wpad[1, 0:32, :] = cst_ref[...]
    wpad[1] = wpad[1].T
    octant_col = wpad[1, 0:GHOST, 9:10]
    lane24 = lax.rem(lax.broadcasted_iota(jnp.int32, (GHOST, 24), 1), 8).astype(F32)
    spread = jnp.where(lane24 == octant_col, 1.0, 0.0).astype(BF16)
    collect = jnp.where(sub8.astype(F32) == cst_ref[9:10, :], 1.0, 0.0).astype(BF16)[:, 0:GHOST]
    pack(0, own[...])
    zeros4 = jnp.zeros((4, 128), F32)
    tile = jnp.concatenate([gram_rows(own, own), zeros4], axis=0)

    pl.semaphore_wait(barrier, len(CELLS) + len(groups[0]) + len(groups[1]))
    copies = halo_send(0, -1)
    ar_send(0, 0, tile)

    atom_lane = lax.broadcasted_iota(jnp.int32, (128, ATOMS), 1).astype(F32)

    def build(j, is_own):
        name = wpad[1, :, j : j + 1]
        for k in range(FAN):
            part = jnp.where(nbr_ref[k].astype(F32) == name, 1.0, 0.0)
            if is_own:
                part = part - jnp.where(atom_lane == name, 1.0, 0.0)
            inc[128 * j : 128 * j + 128, ATOMS * k : ATOMS * k + ATOMS] = part.astype(BF16)

    wpad[0] = jnp.zeros((128, 128), F32)
    hi, mid, lo = (x.astype(F32) for x in split3(rin_ref[...]))
    for n, part in enumerate((hi, mid, lo, hi, mid, hi)):
        wpad[0, 8 * n : 8 * n + 8, :] = part
    wpad[0, 48:50, 0:CH] = emb_ref[...]
    wpad[0, 50:51, 0:CH] = rdo_ref[...]
    wpad[0] = wpad[0].T
    embc[:, 0:3] = wpad[0, 0:CH, 48:51]
    hi, mid, lo = split3(rout_ref[...])
    w2[...] = jnp.concatenate([hi, mid, hi], axis=1)
    epv[...] = jnp.where(own[15:16, :] < 0.5, embc[:, 0:1], embc[:, 1:2])
    for j in range(9):
        build(j, j < 2)
    ar_send(0, 1, ar_recv(0, 0))
    tab[:, 0:256] = own[...]
    halo_wait(copies)
    unpack(0, tab, True)

    def gather(src):
        got = sum3(mm(rows3(src), inc[...]))
        for k in range(FAN):
            dt[:, k, :] = got[:, ATOMS * k : ATOMS * k + ATOMS]

    gather(tab[...])

    d3 = [dt[12 + h] for h in range(3)]
    dist2 = d3[0] * d3[0] + d3[1] * d3[1] + d3[2] * d3[2]
    dist = jnp.sqrt(dist2 + SOFTEN)
    inv_r = 1.0 / dist
    unit = [d * inv_r for d in d3]
    for h in range(3):
        geo[h] = unit[h]
    geo[3] = dist
    geo[4] = inv_r
    geo[5] = dt[15] + own[15:16, :]
    for h in range(3):
        for k in range(FAN):
            row = jnp.broadcast_to(unit[h][k : k + 1, :], (8, ATOMS))
            for l in range(2):
                ub[l, h * FAN + k] = row[:, 128 * l : 128 * l + 128]

    def tangents(product):
        for v in range(4):
            dv = [dt[4 * c + v] for c in range(3)]
            rp = geo[0] * dv[0] + geo[1] * dv[1] + geo[2] * dv[2]
            parts = [rp] + [(dv[h] - geo[h] * rp) * geo[4] for h in range(3)]
            for g in range(4):
                for k in range(FAN):
                    row = jnp.broadcast_to(parts[g][k : k + 1, :], (8, ATOMS))
                    for l in range(2):
                        bv[2 * v + l, g * FAN + k] = row[:, 128 * l : 128 * l + 128]

    tangents(0)

    order8 = (lax.broadcasted_iota(jnp.int32, (8, ATOMS), 0) + 1).astype(F32) * (math.pi / CUTOFF)

    PAIR = 2
    order_w = jnp.concatenate([order8] * PAIR, axis=1)

    def features(pair, z):
        rows = [[geo[n, pl.ds(PAIR * pair + m, 1), :] for m in range(PAIR)] for n in (3, 4, 5)]
        r, ir, kind = (jnp.concatenate(x, axis=1) for x in rows)
        s, c = sin_cos(order_w * r)
        b0 = s * ir
        b1 = (order_w * c - b0) * ir
        b2 = -(order_w * order_w) * b0 - 2.0 * b1 * ir
        rin_t = wpad[0, :, 0:48].astype(BF16)

        def first(b):
            hi, mid, lo = split3(b)
            return mm(rin_t, jnp.concatenate([hi, hi, hi, mid, mid, lo], axis=0))

        def second(h):
            hi = h.astype(BF16)
            mid = (h - hi.astype(F32)).astype(BF16)
            return mm(w2[...], jnp.concatenate([hi, hi, mid], axis=0))

        z0, z1, z2 = first(b0), first(b1), first(b2)
        sg = 1.0 / (1.0 + jnp.exp(-z0))
        sd = sg * (1.0 - sg)
        s1 = sg + z0 * sd
        s2 = sd * (2.0 + z0 * (1.0 - 2.0 * sg))
        r0, r1_, r2 = second(z0 * sg), second(s1 * z1), second(s2 * z1 * z1 + s1 * z2)
        q = r * r * (1.0 / (CUTOFF * CUTOFF))
        sixth = FAN ** -0.5
        e0 = (1.0 - q) * (1.0 - q) * sixth
        e1 = (-4.0 / (CUTOFF * CUTOFF)) * r * (1.0 - q) * sixth
        e2 = (-4.0 / (CUTOFF * CUTOFF)) * (1.0 - 3.0 * q) * sixth
        w = jnp.concatenate([epv[...]] * PAIR, axis=1) * jnp.where(kind < 0.5, embc[:, 0:1], embc[:, 1:2])
        f0 = r0 * e0 * w
        f1 = (r1_ * e0 + r0 * e1) * w
        f2 = (r2 * e0 + 2.0 * r1_ * e1 + r0 * e2) * w
        for slot, val in ((SF, f0), (SF1, f1), (SF2, f2)):
            for m in range(PAIR):
                for l in range(2):
                    for t in range(8):
                        at = ATOMS * m + 128 * l
                        fs[8 * l + t, slot + PAIR * pair + m] = val[8 * t : 8 * t + 8, at : at + 128]
        return z

    lax.fori_loop(0, FAN // PAIR, features, 0)

    ks = range(FAN)
    hs = range(3)

    def base_pass(i, z):
        l = i // 8
        t = lax.rem(i, 8)
        f = [fs[i, SF + k] for k in ks]
        f1 = [fs[i, SF1 + k] for k in ks]
        u = [[ub[l, h * FAN + k] for k in ks] for h in hs]
        rho = jnp.broadcast_to(embc[pl.ds(pl.multiple_of(t * 8, 8), 8), 2:3], (8, 128))
        e0 = sum(f[1:], f[0])
        e = [sum((f[k] * u[h][k] for k in ks[1:]), f[0] * u[h][0]) for h in hs]
        p, a, n = [], [], []
        for k in ks:
            pk = e0 + (e[0] * u[0][k] + e[1] * u[1][k] + e[2] * u[2][k])
            m = f[k] * pk
            sg = 1.0 / (1.0 + jnp.exp(-m))
            sd = sg * (1.0 - sg)
            ak = rho * (sg + m * sd)
            fs[i, SP + k] = pk
            fs[i, SA + k] = ak
            fs[i, SB + k] = rho * (sd * (2.0 + m * (1.0 - 2.0 * sg)))
            p.append(pk)
            a.append(ak)
            n.append(ak * f[k])
        for h in hs:
            fs[i, SE + h] = e[h]
        q0 = sum(n[1:], n[0])
        q = [sum((n[k] * u[h][k] for k in ks[1:]), n[0] * u[h][0]) for h in hs]
        for k in ks:
            fk = a[k] * p[k] + q0 + (q[0] * u[0][k] + q[1] * u[1][k] + q[2] * u[2][k])
            acc[l, k] += fk * f1[k]
            acc[2 + l, k] += fk * fs[i, SF2 + k]
            for h in hs:
                acc[l, FAN * (h + 1) + k] += n[k] * e[h] + f[k] * q[h]
                acc[2 + l, FAN * (h + 1) + k] += f1[k] * q[h]
        return z

    def clear():
        def zero(i, z):
            acc[i] = jnp.zeros((24, 8, 128), F32)
            return z
        lax.fori_loop(0, 8, zero, 0)

    one_row = lax.broadcasted_iota(jnp.int32, (32, 192), 0)
    one_col = lax.broadcasted_iota(jnp.int32, (32, 192), 1) // 8
    ones = jnp.where((one_row % 8 < FAN) & (one_row // 8 * FAN + one_row % 8 == one_col), 1.0, 0.0).astype(BF16)

    def fold(v):
        out = []
        for l in range(2):
            hi, mid, lo = split3(acc[2 * v + l].reshape(192, 128))
            out.append((mm(ones, lo) + mm(ones, mid)) + mm(ones, hi))
        return jnp.concatenate(out, axis=1)

    clear()
    lax.fori_loop(0, 16, base_pass, 0)
    first, second = fold(0), fold(1)
    alpha, beta = first[0:8], second[0:8]
    force = [first[8 * h + 8 : 8 * h + 16] for h in hs]
    cross = [second[8 * h + 8 : 8 * h + 16] for h in hs]
    uv = unit[0] * force[0] + unit[1] * force[1] + unit[2] * force[2]
    sums[0] = alpha
    sums[1] = beta
    sums[2] = uv
    for h in hs:
        sums[3 + h] = force[h]
        sums[6 + h] = cross[h]

    def hvp(i, z):
        v = i // 16
        ch = lax.rem(i, 16)
        vl = 2 * v + ch // 8
        l = ch // 8
        f = [fs[ch, SF + k] for k in ks]
        rp = [bv[vl, k] for k in ks]
        u = lambda h, k: ub[l, h * FAN + k]
        du = lambda h, k: bv[vl, (h + 1) * FAN + k]
        df = [fs[ch, SF1 + k] * rp[k] for k in ks]
        de0 = sum(df[1:], df[0])
        de = []
        for h in hs:
            total = df[0] * u(h, 0) + f[0] * du(h, 0)
            for k in ks[1:]:
                total = total + (df[k] * u(h, k) + f[k] * du(h, k))
            de.append(total)
        e = [fs[ch, SE + h] for h in hs]
        dn, dfeat, n = [], [], []
        for k in ks:
            dp = de0
            for h in hs:
                dp = dp + (de[h] * u(h, k) + e[h] * du(h, k))
            pk, ak = fs[ch, SP + k], fs[ch, SA + k]
            da = fs[ch, SB + k] * (df[k] * pk + f[k] * dp)
            dn.append(da * f[k] + ak * df[k])
            n.append(ak * f[k])
            dfeat.append(da * pk + ak * dp)
        dq0 = sum(dn[1:], dn[0])
        dq = []
        for h in hs:
            total = dn[0] * u(h, 0) + n[0] * du(h, 0)
            for k in ks[1:]:
                total = total + (dn[k] * u(h, k) + n[k] * du(h, k))
            dq.append(total)
        for k in ks:
            tot = dfeat[k] + dq0 + (dq[0] * u(0, k) + dq[1] * u(1, k) + dq[2] * u(2, k))
            acc[vl, k] += fs[ch, SF1 + k] * tot
            for h in hs:
                acc[vl, FAN * (h + 1) + k] += (dn[k] * e[h] + n[k] * de[h]) + f[k] * dq[h]
        return z

    grs[12:16] = jnp.zeros((4, 8, ATOMS), F32)

    def finish_hvp():
        u3 = [geo[h] for h in hs]
        ir = geo[4]
        for v in range(4):
            got = fold(v)
            dv = [dt[4 * c + v] for c in range(3)]
            rp = u3[0] * dv[0] + u3[1] * dv[1] + u3[2] * dv[2]
            du = [(dv[h] - u3[h] * rp) * ir for h in hs]
            al, be, w0 = sums[0], sums[1], sums[2]
            fo = [sums[3 + h] for h in hs]
            cr = [sums[6 + h] for h in hs]
            dal = got[0:8] + be * rp + (cr[0] * du[0] + cr[1] * du[1] + cr[2] * du[2])
            dfo = [got[8 * h + 8 : 8 * h + 16] + rp * cr[h] for h in hs]
            duv = sum((du[h] * fo[h] + u3[h] * dfo[h] for h in hs[1:]), du[0] * fo[0] + u3[0] * dfo[0])
            back = rp * ir
            for h in hs:
                val = dal * u3[h] + al * du[h]
                val = val + ir * ((dfo[h] - du[h] * w0 - u3[h] * duv) - back * (fo[h] - u3[h] * w0))
                grs[4 * h + v] = val
        for k in ks:
            cb[:, ATOMS * k : ATOMS * k + ATOMS] = rows3(grs[:, k, :])

    def scatter(at):
        return sum3(mm(cb[...], inc[at, :], ((1,), (1,))))

    def give_back(i):
        finish_hvp()
        pack_back(i, scatter(pl.ds(256, COLS - 256)))
        copies = halo_send(i, 1)
        return copies, scatter(pl.ds(0, 256))

    def combine_all(dst, cols, src, minus=None):
        for c in range(3):
            got = combine(cols, src, c)
            dst[4 * c : 4 * c + 4, :] = got if minus is None else minus[4 * c : 4 * c + 4, :] - got

    def transposed(proj):
        return [place([proj[u][w] for w in range(4)]) for u in range(4)]

    clear()
    lax.fori_loop(0, 64, hvp, 0)
    low, inv = cholesky(entries(ar_recv(0, 1), 0))
    cols0 = columns_of(inv)
    copies, local = give_back(1)
    combine_all(v1, cols0, own)
    w1[12:16, :] = jnp.zeros((4, ATOMS), F32)
    halo_wait(copies)
    own[...] = local + unpack_back(1)
    combine_all(w1, cols0, own)
    pack(2, w1[...])
    copies = halo_send(2, -1)
    ar_send(1, 0, jnp.concatenate([gram_rows(v1, w1), zeros4], axis=0))
    tab[:, 0:256] = w1[...]
    clear()
    ar_send(1, 1, ar_recv(1, 0))
    halo_wait(copies)
    unpack(2, tab, False)

    gather(tab[...])
    tangents(1)
    lax.fori_loop(0, 16, hvp, 0)
    proj = entries(ar_recv(1, 1), 0)
    cols_a = transposed(proj)
    combine_all(r1, cols_a, v1, w1)
    ar_send(2, 0, jnp.concatenate([gram_rows(r1, r1), zeros4], axis=0))
    diag_ref[0] = matrix(lambda u, w: proj[u][w])
    lax.fori_loop(16, 64, hvp, 0)
    ar_send(2, 1, ar_recv(2, 0))
    copies, local = give_back(3)
    low, inv = cholesky(entries(ar_recv(2, 1), 0))
    cols1 = columns_of(inv)
    off_ref[0] = matrix(lambda u, w: low[w][u] if w >= u else None)
    combine_all(v2, cols1, r1)
    halo_wait(copies)
    own[...] = local + unpack_back(3)
    combine_all(r1, cols_a, w1, own)
    combine_all(own, cols1, r1)
    gram_w = pltpu.roll(jnp.concatenate([gram_rows(own, own), zeros4], axis=0), 4, 1)
    tile = jnp.concatenate([gram_rows(v2, own), gram_rows(v1, own)], axis=0) + gram_w
    for g in range(2):
        ar_send(3, g, tile)
        tile = ar_recv(3, g)
    proj = entries(tile, 0)
    prev = entries(tile, 4)
    gram = entries(pltpu.roll(tile, 124, 1), 0)
    for u in range(4):
        for w in range(u + 1):
            total = gram[u][w]
            for m in range(4):
                total = total - (proj[m][u] * proj[m][w] + prev[m][u] * prev[m][w])
            gram[u][w] = total
    combine_all(r1, transposed(proj), v2, own)
    combine_all(own, transposed(prev), v1, r1)
    low, inv = cholesky(gram)
    cols = columns_of(inv)
    for c in range(3):
        next_ref[c] = combine(cols, own, c)
    diag_ref[1] = matrix(lambda u, w: proj[u][w])
    off_ref[1] = matrix(lambda u, w: low[w][u] if w >= u else None)
    for copy in pending:
        copy.wait_send()


def solution(mesh):
    sizes = tuple(mesh.shape[a] for a in AXES)
    cst = constants()
    slots = 2 * sizes[0] + sizes[1] * sizes[2] // 2

    def on_device(positions, species, start_block, neighbors, ghost_lists, embedding, radial_in, radial_out, readout):
        vmem = pl.BlockSpec(memory_space=pltpu.VMEM)
        vm = lambda *shape: pltpu.VMEM(shape, F32)
        dma = lambda *shape: pltpu.SemaphoreType.DMA(shape)
        out = pl.pallas_call(
            functools.partial(kernel, sizes),
            out_shape=(
                jax.ShapeDtypeStruct((3, 4, ATOMS), F32),
                jax.ShapeDtypeStruct((2, 4, 4), F32),
                jax.ShapeDtypeStruct((2, 4, 4), F32),
            ),
            in_specs=[vmem] * 10,
            out_specs=(vmem, vmem, vmem),
            scratch_shapes=[
                vm(ROWS, ATOMS),
                pltpu.VMEM((COLS, FAN * ATOMS), BF16),
                vm(ROWS, COLS),
                vm(ROWS, ATOMS), vm(ROWS, ATOMS), vm(ROWS, ATOMS), vm(ROWS, ATOMS),
                vm(ROWS, 8, ATOMS), vm(ROWS, 8, ATOMS),
                vm(6, 8, ATOMS), vm(9, 8, ATOMS),
                vm(2, 18, 8, 128), vm(8, 24, 8, 128),
                vm(16, 39, 8, 128), vm(8, 24, 8, 128),
                vm(CH, ATOMS), vm(2, 128, 128),
                pltpu.VMEM((CH, 3 * HID), BF16), vm(CH, 128),
                pltpu.VMEM((ATOMS, 128), BF16), pltpu.VMEM((8, 128), jnp.int32),
                pltpu.VMEM((3 * ROWS, FAN * ATOMS), BF16),
                vm(4, GHOST, 256), vm(4, GHOST, 256),
                vm(4, slots, 8, 128),
                dma(4, 26), dma(4, 26), dma(4, slots), dma(4, slots),
            ],
            compiler_params=pltpu.CompilerParams(
                collective_id=0, has_side_effects=True, vmem_limit_bytes=48 * 1024 * 1024
            ),
        )(
            positions.reshape(3, 1, ATOMS), species.reshape(1, ATOMS),
            jnp.transpose(start_block[0, 0, 0], (1, 0, 2)), neighbors.reshape(FAN, 1, ATOMS),
            ghost_lists, embedding, radial_in, radial_out.T, readout[None], jnp.asarray(cst),
        )
        return jnp.transpose(out[0], (1, 0, 2))[None, None, None], out[1], out[2]

    return jax.shard_map(
        on_device,
        mesh=mesh,
        in_specs=(
            P("gx", "gy", "gz", None, None),
            P("gx", "gy", "gz", None),
            P("gx", "gy", "gz", None, None, None),
            P("gx", "gy", "gz", None, None),
            P("gx", "gy", "gz", None),
            P(), P(), P(), P(),
        ),
        out_specs=(P("gx", "gy", "gz", None, None, None), P(), P()),
        check_vma=False,
    )
```

time: 106 us -> 73.1 us (0.69)
  Pallas kernels: 97.8 us -> 64.7 us
    pallas_call x1, Pallas kernels: 97.8 us -> 64.7 us  [on_device(): pl.pallas_call(functools.partial(kernel, sizes), out_shape=(jax.ShapeDtyp...]
    unnamed x23, local copies, waits for them, and re-layouts: 5.7 us -> 7.36 us
where the time goes in v2:
time: 73.1 us; the launch traced here: 72.7 us
  Pallas kernels  64.7 us (89%)
  local copies, waits for them, and re-layouts  7.36 us (10%)
    pallas_call x1, Pallas kernels, on_device(): pl.pallas_call(functools.partial(kernel, sizes), out_shape=(jax.ShapeDtyp...  64.7 us
    unnamed x23, local copies, waits for them, and re-layouts  7.36 us

profile of v2, /device:TPU:1, one launch (start us, length us, event | category | flops | bytes accessed | tf_op | source)
XLA Modules:
  0.0 72.7 jit_solution(13965874027326302202)
XLA Ops:
  0.6 0.0 copy-start.3
  0.6 0.0 copy-start.4
  0.7 0.0 copy-start.7
  0.7 0.7 copy-done.3
  1.3 0.0 copy-done.4
  1.3 0.0 copy-done.7
  1.3 0.0 copy-start
  1.3 0.8 %copy-done = f32[128,64]{0,1:T(8,128)S(1)} copy-done((f32[128,64]{0,1:T(8,128)S(1)}, f32[128,64]{0,1:T(8,128)}, u32[]{:S(2)}) %copy-start) | copy-done | bytes 32792
  2.1 0.0 copy-start.1
  2.1 0.7 copy-done.1
  2.8 0.0 copy-start.2
  2.8 0.7 copy-done.2
  3.5 0.0 copy-start.5
  3.5 0.7 copy-done.5
  4.2 0.0 copy-start.6
  4.2 0.7 copy-done.6
  4.9 0.0 copy-start.8
  4.9 0.7 copy-done.8
  5.6 0.0 copy-start.9
  5.6 0.7 copy-done.9
  6.2 64.7 %shard_map.121 = (f32[3,4,256]{2,1,0:T(4,128)S(1)}, f32[2,4,4]{2,1,0:T(4,128)S(1)}, f32[2,4,4]{2,1,0:T(4,128)S(1)}) custom-call(f32[3,1,256]{2,1,0:T(1,128)S(1)} %bitcast.15, s32[1,256]{1,0:T(1,128)S(1)} %bitcast.16, f32[3,4,256]{2,1,0:T(4,128)S(1)} %bitcast.12, s32[6,1,256]{2,1,0:T(1,128)S(1)} %bitcast.14, s32[2,2,2,16]{3,2,1,0:T(2,128)S(1)} %copy-done.4, ...), custom_call_target="tpu_custom_call" | custom-call | tf_op jit(solution)/shard_map/pallas_call | solution.py:665
  70.9 0.6 copy.16
  71.5 0.6 copy.17
  72.1 0.6 copy.18
Async XLA Ops:
  0.6 0.7 copy-start.3
  0.6 0.7 copy-start.4
  0.7 0.7 copy-start.7
  1.3 0.8 %copy-start = (f32[128,64]{0,1:T(8,128)S(1)}, f32[128,64]{0,1:T(8,128)}, u32[]{:S(2)}) copy-start(f32[128,64]{0,1:T(8,128)} %param.17) | copy-start | bytes 98308
  2.1 0.7 copy-start.1
  2.8 0.7 copy-start.2
  3.5 0.7 copy-start.5
  4.2 0.7 copy-start.6
  4.9 0.7 copy-start.8
  5.6 0.7 copy-start.9

commit v3 on v2

--- a/solution.py
+++ b/solution.py
@@ -110,11 +110,18 @@
 
 
 def kernel(
-    sizes, pos_ref, spc_ref, sb_ref, nbr_ref, gl_ref, emb_ref, rin_ref, rout_ref, rdo_ref, cst_ref,
-    next_ref, diag_ref, off_ref,
-    own, inc, tab, v1, w1, r1, v2, dt, grs, geo, sums, ub, bv, fs, acc, epv, wpad, w2, embc, ghost, glw, cb,
-    hs_buf, hr_buf, arb, hsend, hrecv, asend, arecv,
+    sizes, *refs,
 ):
+    hbm, (next_ref, diag_ref, off_ref) = refs[:10], refs[10:13]
+    arrived, *local = refs[13:24]
+    pos_ref, spc_ref, sb_ref, nbr_ref, gl_ref, emb_ref, rin_ref, rout_ref, rdo_ref, cst_ref = local
+    (
+        own, inc, inc_t, tab, v1, w1, r1, v2, dt, grs, geo, sums, ub, bv, fs, acc, epv, wpad, w2, embc, ghost, glw, cb,
+        hs_buf, hr_buf, arb, hsend, hrecv, asend, arecv,
+    ) = refs[24:]
+    fetch = [pltpu.make_async_copy(a, b, arrived.at[n]) for n, (a, b) in enumerate(zip(hbm, local))]
+    for copy in fetch:
+        copy.start()
     gx, gy, gz = (lax.axis_index(a) for a in AXES)
     scale_ip = 1.0 / (3.0 * ATOMS * sizes[0] * sizes[1] * sizes[2])
 
@@ -148,51 +155,47 @@
     lane8 = lax.broadcasted_iota(jnp.int32, (8, 128), 1)
     sub8 = lax.broadcasted_iota(jnp.int32, (8, 128), 0)
 
-    pending = []
-
     def ar_send(i, g, tile):
         mine = starts[g] + partner((0,) * 5)[1][g]
         arb[i, mine] = tile
-        for n, o in enumerate(groups[g]):
-            copy = pltpu.make_async_remote_copy(
+        for o in groups[g]:
+            pltpu.make_async_remote_copy(
                 src_ref=arb.at[i, mine], dst_ref=arb.at[i, mine],
-                send_sem=asend.at[i, starts[g] + n], recv_sem=arecv.at[i, mine],
+                send_sem=asend.at[i, g], recv_sem=arecv.at[i, g],
                 device_id=partner(o)[0], device_id_type=MESH,
-            )
-            copy.start()
-            pending.append(copy)
+            ).start()
+
+    def ar_all(i, g):
+        part = arb.at[i, pl.ds(starts[g], len(groups[g]))]
+        return pltpu.make_async_remote_copy(
+            src_ref=part, dst_ref=part, send_sem=asend.at[i, g], recv_sem=arecv.at[i, g],
+            device_id=partner(groups[g][0])[0], device_id_type=MESH,
+        )
 
     def ar_recv(i, g):
-        for n, o in enumerate(groups[g]):
-            device, at = partner(o)
-            src = starts[g] + at[g]
-            pltpu.make_async_remote_copy(
-                src_ref=arb.at[i, src], dst_ref=arb.at[i, src],
-                send_sem=asend.at[i, starts[g] + n], recv_sem=arecv.at[i, src],
-                device_id=device, device_id_type=MESH,
-            ).wait_recv()
+        ar_all(i, g).wait_recv()
         parts = [arb[i, starts[g] + j] for j in range(len(groups[g]) + 1)]
         while len(parts) > 1:
             parts = [a + b for a, b in zip(parts[::2], parts[1::2])] + parts[len(parts) // 2 * 2 :]
         return parts[0]
 
     def halo_send(i, sign):
-        copies = []
-        for n, (s, first, octants) in enumerate(CELLS):
+        for s, first, octants in CELLS:
             at = pl.ds(first, len(octants))
-            copy = pltpu.make_async_remote_copy(
+            pltpu.make_async_remote_copy(
                 src_ref=hs_buf.at[i, at], dst_ref=hr_buf.at[i, at],
-                send_sem=hsend.at[i, n], recv_sem=hrecv.at[i, n],
+                send_sem=hsend.at[i], recv_sem=hrecv.at[i],
                 device_id=beside(tuple(sign * x for x in s)), device_id_type=MESH,
-            )
-            copy.start()
-            copies.append(copy)
-        pending.extend(copies)
-        return copies
-
-    def halo_wait(copies):
-        for copy in copies:
-            copy.wait_recv()
+            ).start()
+
+    def halo_all(i):
+        return pltpu.make_async_remote_copy(
+            src_ref=hs_buf.at[i], dst_ref=hr_buf.at[i], send_sem=hsend.at[i], recv_sem=hrecv.at[i],
+            device_id=beside(CELLS[0][0]), device_id_type=MESH,
+        )
+
+    def halo_wait(i):
+        halo_all(i).wait_recv()
 
     def turn(x):
         for b in (2, 1, 0):
@@ -298,6 +301,9 @@
             total = total + cols[w] * src[4 * c + w : 4 * c + w + 1, :]
         return total
 
+    for copy in fetch:
+        copy.wait()
+
     for c in range(3):
         own[4 * c : 4 * c + 4, :] = sb_ref[c]
         own[12 + c : 13 + c, :] = pos_ref[c]
@@ -322,7 +328,7 @@
     tile = jnp.concatenate([gram_rows(own, own), zeros4], axis=0)
 
     pl.semaphore_wait(barrier, len(CELLS) + len(groups[0]) + len(groups[1]))
-    copies = halo_send(0, -1)
+    halo_send(0, -1)
     ar_send(0, 0, tile)
 
     atom_lane = lax.broadcasted_iota(jnp.int32, (128, ATOMS), 1).astype(F32)
@@ -334,6 +340,18 @@
             if is_own:
                 part = part - jnp.where(atom_lane == name, 1.0, 0.0)
             inc[128 * j : 128 * j + 128, ATOMS * k : ATOMS * k + ATOMS] = part.astype(BF16)
+
+    atom_sub = lax.broadcasted_iota(jnp.int32, (128, 128), 0).astype(F32)
+
+    def build_t(k, l):
+        at = pl.ds(ATOMS * k + 128 * l, 128)
+        name = wpad[2 + l, :, k : k + 1]
+        for j in range(9):
+            entry = cst_ref[j : j + 1, :]
+            part = jnp.where(entry == name, 1.0, 0.0)
+            if j < 2:
+                part = part - jnp.where(atom_sub + 128.0 * l == entry, 1.0, 0.0)
+            inc_t[at, 128 * j : 128 * j + 128] = part.astype(BF16)
 
     wpad[0] = jnp.zeros((128, 128), F32)
     hi, mid, lo = (x.astype(F32) for x in split3(rin_ref[...]))
@@ -346,11 +364,19 @@
     hi, mid, lo = split3(rout_ref[...])
     w2[...] = jnp.concatenate([hi, mid, hi], axis=1)
     epv[...] = jnp.where(own[15:16, :] < 0.5, embc[:, 0:1], embc[:, 1:2])
+    for l in range(2):
+        wpad[2 + l] = jnp.zeros((128, 128), F32)
+        for k in range(FAN):
+            wpad[2 + l, k : k + 1, :] = nbr_ref[k, :, 128 * l : 128 * l + 128].astype(F32)
+        wpad[2 + l] = wpad[2 + l].T
     for j in range(9):
         build(j, j < 2)
+    for k in range(FAN):
+        for l in range(2):
+            build_t(k, l)
     ar_send(0, 1, ar_recv(0, 0))
     tab[:, 0:256] = own[...]
-    halo_wait(copies)
+    halo_wait(0)
     unpack(0, tab, True)
 
     def gather(src):
@@ -391,7 +417,7 @@
 
     order8 = (lax.broadcasted_iota(jnp.int32, (8, ATOMS), 0) + 1).astype(F32) * (math.pi / CUTOFF)
 
-    PAIR = 2
+    PAIR = 3
     order_w = jnp.concatenate([order8] * PAIR, axis=1)
 
     def features(pair, z):
@@ -493,7 +519,7 @@
         return jnp.concatenate(out, axis=1)
 
     clear()
-    lax.fori_loop(0, 16, base_pass, 0)
+    lax.fori_loop(0, 16, base_pass, 0, unroll=2)
     first, second = fold(0), fold(1)
     alpha, beta = first[0:8], second[0:8]
     force = [first[8 * h + 8 : 8 * h + 16] for h in hs]
@@ -573,13 +599,13 @@
             cb[:, ATOMS * k : ATOMS * k + ATOMS] = rows3(grs[:, k, :])
 
     def scatter(at):
-        return sum3(mm(cb[...], inc[at, :], ((1,), (1,))))
+        return sum3(mm(cb[...], inc_t[:, at]))
 
     def give_back(i):
         finish_hvp()
         pack_back(i, scatter(pl.ds(256, COLS - 256)))
-        copies = halo_send(i, 1)
-        return copies, scatter(pl.ds(0, 256))
+        halo_send(i, 1)
+        return scatter(pl.ds(0, 256))
 
     def combine_all(dst, cols, src, minus=None):
         for c in range(3):
@@ -590,40 +616,45 @@
         return [place([proj[u][w] for w in range(4)]) for u in range(4)]
 
     clear()
-    lax.fori_loop(0, 64, hvp, 0)
+    lax.fori_loop(0, 64, hvp, 0, unroll=2)
     low, inv = cholesky(entries(ar_recv(0, 1), 0))
     cols0 = columns_of(inv)
-    copies, local = give_back(1)
+    local = give_back(1)
     combine_all(v1, cols0, own)
     w1[12:16, :] = jnp.zeros((4, ATOMS), F32)
-    halo_wait(copies)
+    halo_wait(1)
     own[...] = local + unpack_back(1)
     combine_all(w1, cols0, own)
     pack(2, w1[...])
-    copies = halo_send(2, -1)
+    halo_send(2, -1)
     ar_send(1, 0, jnp.concatenate([gram_rows(v1, w1), zeros4], axis=0))
     tab[:, 0:256] = w1[...]
     clear()
     ar_send(1, 1, ar_recv(1, 0))
-    halo_wait(copies)
+    halo_wait(2)
     unpack(2, tab, False)
 
     gather(tab[...])
     tangents(1)
-    lax.fori_loop(0, 16, hvp, 0)
+    lax.fori_loop(0, 16, hvp, 0, unroll=2)
     proj = entries(ar_recv(1, 1), 0)
     cols_a = transposed(proj)
     combine_all(r1, cols_a, v1, w1)
     ar_send(2, 0, jnp.concatenate([gram_rows(r1, r1), zeros4], axis=0))
     diag_ref[0] = matrix(lambda u, w: proj[u][w])
-    lax.fori_loop(16, 64, hvp, 0)
+    lax.fori_loop(16, 64, hvp, 0, unroll=2)
     ar_send(2, 1, ar_recv(2, 0))
-    copies, local = give_back(3)
+    local = give_back(3)
     low, inv = cholesky(entries(ar_recv(2, 1), 0))
     cols1 = columns_of(inv)
     off_ref[0] = matrix(lambda u, w: low[w][u] if w >= u else None)
     combine_all(v2, cols1, r1)
-    halo_wait(copies)
+    for i in range(4):
+        halo_all(i).wait_send()
+    for i in range(3):
+        for g in range(2):
+            ar_all(i, g).wait_send()
+    halo_wait(3)
     own[...] = local + unpack_back(3)
     combine_all(r1, cols_a, w1, own)
     combine_all(own, cols1, r1)
@@ -649,8 +680,8 @@
         next_ref[c] = combine(cols, own, c)
     diag_ref[1] = matrix(lambda u, w: proj[u][w])
     off_ref[1] = matrix(lambda u, w: low[w][u] if w >= u else None)
-    for copy in pending:
-        copy.wait_send()
+    for g in range(2):
+        ar_all(3, g).wait_send()
 
 
 def solution(mesh):
@@ -662,6 +693,11 @@
         vmem = pl.BlockSpec(memory_space=pltpu.VMEM)
         vm = lambda *shape: pltpu.VMEM(shape, F32)
         dma = lambda *shape: pltpu.SemaphoreType.DMA(shape)
+        operands = (
+            positions.reshape(3, 1, ATOMS), species.reshape(1, ATOMS),
+            jnp.transpose(start_block[0, 0, 0], (1, 0, 2)), neighbors.reshape(FAN, 1, ATOMS),
+            ghost_lists, embedding, radial_in, radial_out.T, readout[None], jnp.asarray(cst),
+        )
         out = pl.pallas_call(
             functools.partial(kernel, sizes),
             out_shape=(
@@ -669,33 +705,32 @@
                 jax.ShapeDtypeStruct((2, 4, 4), F32),
                 jax.ShapeDtypeStruct((2, 4, 4), F32),
             ),
-            in_specs=[vmem] * 10,
+            in_specs=[pl.BlockSpec(memory_space=pltpu.HBM)] * 10,
             out_specs=(vmem, vmem, vmem),
-            scratch_shapes=[
+            scratch_shapes=[dma(10)]
+            + [pltpu.VMEM(x.shape, x.dtype) for x in operands]
+            + [
                 vm(ROWS, ATOMS),
                 pltpu.VMEM((COLS, FAN * ATOMS), BF16),
+                pltpu.VMEM((FAN * ATOMS, COLS), BF16),
                 vm(ROWS, COLS),
                 vm(ROWS, ATOMS), vm(ROWS, ATOMS), vm(ROWS, ATOMS), vm(ROWS, ATOMS),
                 vm(ROWS, 8, ATOMS), vm(ROWS, 8, ATOMS),
                 vm(6, 8, ATOMS), vm(9, 8, ATOMS),
                 vm(2, 18, 8, 128), vm(8, 24, 8, 128),
                 vm(16, 39, 8, 128), vm(8, 24, 8, 128),
-                vm(CH, ATOMS), vm(2, 128, 128),
+                vm(CH, ATOMS), vm(4, 128, 128),
                 pltpu.VMEM((CH, 3 * HID), BF16), vm(CH, 128),
                 pltpu.VMEM((ATOMS, 128), BF16), pltpu.VMEM((8, 128), jnp.int32),
                 pltpu.VMEM((3 * ROWS, FAN * ATOMS), BF16),
                 vm(4, GHOST, 256), vm(4, GHOST, 256),
                 vm(4, slots, 8, 128),
-                dma(4, 26), dma(4, 26), dma(4, slots), dma(4, slots),
+                dma(4), dma(4), dma(4, 2), dma(4, 2),
             ],
             compiler_params=pltpu.CompilerParams(
-                collective_id=0, has_side_effects=True, vmem_limit_bytes=48 * 1024 * 1024
+                collective_id=0, has_side_effects=True, vmem_limit_bytes=67_043_328
             ),
-        )(
-            positions.reshape(3, 1, ATOMS), species.reshape(1, ATOMS),
-            jnp.transpose(start_block[0, 0, 0], (1, 0, 2)), neighbors.reshape(FAN, 1, ATOMS),
-            ghost_lists, embedding, radial_in, radial_out.T, readout[None], jnp.asarray(cst),
-        )
+        )(*operands)
         return jnp.transpose(out[0], (1, 0, 2))[None, None, None], out[1], out[2]
 
     return jax.shard_map(

time: 73.1 us -> 63.5 us (0.87)
  local copies, waits for them, and re-layouts: 7.36 us -> 2.58 us
  Pallas kernels: 64.7 us -> 60 us
    unnamed x23 -> x7, local copies, waits for them, and re-layouts: 7.36 us -> 2.58 us
    pallas_call x1, Pallas kernels: 64.7 us -> 60 us  [on_device(): pl.pallas_call(functools.partial(kernel, sizes), out_shape=(jax.ShapeDtyp...]
where the time goes in v3:
time: 63.5 us; the launch traced here: 63.2 us
  Pallas kernels  60 us (94%)
  local copies, waits for them, and re-layouts  2.58 us (4%)
  between operations  0.65 us (1%)
    pallas_call x1, Pallas kernels, on_device(): pl.pallas_call(functools.partial(kernel, sizes), out_shape=(jax.ShapeDtyp...  60 us
    unnamed x7, local copies, waits for them, and re-layouts  2.58 us

profile of v3, /device:TPU:1, one launch (start us, length us, event | category | flops | bytes accessed | tf_op | source)
XLA Modules:
  0.0 63.2 jit_solution(18097970922377620729)
XLA Ops:
  0.6 60.0 %shard_map.121 = (f32[3,4,256]{2,1,0:T(4,128)}, f32[2,4,4]{2,1,0:T(4,128)}, f32[2,4,4]{2,1,0:T(4,128)}) custom-call(f32[3,1,256]{2,1,0:T(1,128)} %bitcast.15, s32[1,256]{1,0:T(1,128)} %bitcast.16, f32[3,4,256]{2,1,0:T(4,128)} %bitcast.12, s32[6,1,256]{2,1,0:T(1,128)} %bitcast.14, s32[2,2,2,16]{3,2,1,0:T(2,128)} %refs_4_.1, f32[2,64]{1,0:T(2,128)} %refs_5_.1, ...), custom_call_target="tpu_custom_call" | custom-call | tf_op jit(solution)/shard_map/pallas_call | solution.py:701
  60.6 0.0 copy-start.1
  60.6 1.3 %copy.16 = f32[1,1,1,4,3,256]{5,3,4,2,1,0:T(4,128)} copy(f32[1,1,1,4,3,256]{5,3,4,2,1,0:T(4,128)} %bitcast.13) | data formatting | bytes 24576
  61.9 0.0 copy-done.1
  61.9 0.0 copy-start
  61.9 0.6 copy.17
  62.5 0.1 copy-done
  62.6 0.6 copy.18
Async XLA Ops:
  60.6 1.3 %copy-start.1 = (f32[2,4,4]{2,1,0:T(4,128)S(1)}, f32[2,4,4]{2,1,0:T(4,128)}, u32[]{:S(2)}) copy-start(f32[2,4,4]{2,1,0:T(4,128)} %get-tuple-element.13) | copy-start | bytes 388
  61.9 0.7 %copy-start = (f32[2,4,4]{2,1,0:T(4,128)S(1)}, f32[2,4,4]{2,1,0:T(4,128)}, u32[]{:S(2)}) copy-start(f32[2,4,4]{2,1,0:T(4,128)} %get-tuple-element.14) | copy-start | bytes 388

commit v4 on v3

--- a/solution.py
+++ b/solution.py
@@ -25,7 +25,7 @@
 HIGHEST = lax.Precision.HIGHEST
 MESH = pl.DeviceIdType.MESH
 
-SF, SF1, SF2, SP, SA, SB, SE = 0, 6, 12, 18, 24, 30, 36
+SF, SF1, SF2, SP, SA, SB, SE, SN, SBP = 0, 6, 12, 18, 24, 30, 36, 39, 45
 
 
 def neighbour_cells():
@@ -112,13 +112,13 @@
 def kernel(
     sizes, *refs,
 ):
-    hbm, (next_ref, diag_ref, off_ref) = refs[:10], refs[10:13]
-    arrived, *local = refs[13:24]
+    hbm, (next_ref, small_ref) = refs[:10], refs[10:12]
+    arrived, *local = refs[12:23]
     pos_ref, spc_ref, sb_ref, nbr_ref, gl_ref, emb_ref, rin_ref, rout_ref, rdo_ref, cst_ref = local
     (
         own, inc, inc_t, tab, v1, w1, r1, v2, dt, grs, geo, sums, ub, bv, fs, acc, epv, wpad, w2, embc, ghost, glw, cb,
         hs_buf, hr_buf, arb, hsend, hrecv, asend, arecv,
-    ) = refs[24:]
+    ) = refs[23:]
     fetch = [pltpu.make_async_copy(a, b, arrived.at[n]) for n, (a, b) in enumerate(zip(hbm, local))]
     for copy in fetch:
         copy.start()
@@ -145,8 +145,11 @@
         e = lax.rem(lax.rem(gz, 2) + o[4], 2)
         return {"gx": 2 * a + b, "gy": c, "gz": 2 * d + e}, (4 * a + 2 * b + e, nz * c + d)
 
+    far = sorted(CELLS, key=lambda x: -(5 * abs(x[0][2]) + 2 * abs(x[0][1]) + abs(x[0][0])))
+    for group in groups:
+        group.sort(key=lambda o: -(min(o[2], ny - o[2]) + min(o[3], nz - o[3]) + o[0] + 2 * o[4]))
     barrier = pltpu.get_barrier_semaphore()
-    for s, _, _ in CELLS:
+    for s, _, _ in far:
         pl.semaphore_signal(barrier, inc=1, device_id=beside(s), device_id_type=MESH)
     for group in groups:
         for o in group:
@@ -180,7 +183,7 @@
         return parts[0]
 
     def halo_send(i, sign):
-        for s, first, octants in CELLS:
+        for s, first, octants in far:
             at = pl.ds(first, len(octants))
             pltpu.make_async_remote_copy(
                 src_ref=hs_buf.at[i, at], dst_ref=hr_buf.at[i, at],
@@ -275,8 +278,8 @@
             total = g[j][j]
             for m in range(j):
                 total = total - low[j][m] * low[j][m]
-            low[j][j] = jnp.sqrt(total)
-            inv_d[j] = 1.0 / low[j][j]
+            inv_d[j] = lax.rsqrt(total)
+            low[j][j] = total * inv_d[j]
             for u in range(j + 1, 4):
                 total = g[u][j]
                 for m in range(j):
@@ -484,10 +487,14 @@
             ak = rho * (sg + m * sd)
             fs[i, SP + k] = pk
             fs[i, SA + k] = ak
-            fs[i, SB + k] = rho * (sd * (2.0 + m * (1.0 - 2.0 * sg)))
+            bk = rho * (sd * (2.0 + m * (1.0 - 2.0 * sg)))
+            nk = ak * f[k]
+            fs[i, SB + k] = bk * f[k]
+            fs[i, SBP + k] = bk * (f1[k] * pk)
+            fs[i, SN + k] = nk
             p.append(pk)
             a.append(ak)
-            n.append(ak * f[k])
+            n.append(nk)
         for h in hs:
             fs[i, SE + h] = e[h]
         q0 = sum(n[1:], n[0])
@@ -556,9 +563,9 @@
             for h in hs:
                 dp = dp + (de[h] * u(h, k) + e[h] * du(h, k))
             pk, ak = fs[ch, SP + k], fs[ch, SA + k]
-            da = fs[ch, SB + k] * (df[k] * pk + f[k] * dp)
+            da = fs[ch, SBP + k] * rp[k] + fs[ch, SB + k] * dp
             dn.append(da * f[k] + ak * df[k])
-            n.append(ak * f[k])
+            n.append(fs[ch, SN + k])
             dfeat.append(da * pk + ak * dp)
         dq0 = sum(dn[1:], dn[0])
         dq = []
@@ -641,13 +648,13 @@
     cols_a = transposed(proj)
     combine_all(r1, cols_a, v1, w1)
     ar_send(2, 0, jnp.concatenate([gram_rows(r1, r1), zeros4], axis=0))
-    diag_ref[0] = matrix(lambda u, w: proj[u][w])
+    small_ref[0] = matrix(lambda u, w: proj[u][w])
     lax.fori_loop(16, 64, hvp, 0, unroll=2)
     ar_send(2, 1, ar_recv(2, 0))
     local = give_back(3)
     low, inv = cholesky(entries(ar_recv(2, 1), 0))
     cols1 = columns_of(inv)
-    off_ref[0] = matrix(lambda u, w: low[w][u] if w >= u else None)
+    small_ref[2] = matrix(lambda u, w: low[w][u] if w >= u else None)
     combine_all(v2, cols1, r1)
     for i in range(4):
         halo_all(i).wait_send()
@@ -678,8 +685,8 @@
     cols = columns_of(inv)
     for c in range(3):
         next_ref[c] = combine(cols, own, c)
-    diag_ref[1] = matrix(lambda u, w: proj[u][w])
-    off_ref[1] = matrix(lambda u, w: low[w][u] if w >= u else None)
+    small_ref[1] = matrix(lambda u, w: proj[u][w])
+    small_ref[3] = matrix(lambda u, w: low[w][u] if w >= u else None)
     for g in range(2):
         ar_all(3, g).wait_send()
 
@@ -702,11 +709,10 @@
             functools.partial(kernel, sizes),
             out_shape=(
                 jax.ShapeDtypeStruct((3, 4, ATOMS), F32),
-                jax.ShapeDtypeStruct((2, 4, 4), F32),
-                jax.ShapeDtypeStruct((2, 4, 4), F32),
+                jax.ShapeDtypeStruct((4, 4, 4), F32),
             ),
             in_specs=[pl.BlockSpec(memory_space=pltpu.HBM)] * 10,
-            out_specs=(vmem, vmem, vmem),
+            out_specs=(vmem, vmem),
             scratch_shapes=[dma(10)]
             + [pltpu.VMEM(x.shape, x.dtype) for x in operands]
             + [
@@ -718,7 +724,7 @@
                 vm(ROWS, 8, ATOMS), vm(ROWS, 8, ATOMS),
                 vm(6, 8, ATOMS), vm(9, 8, ATOMS),
                 vm(2, 18, 8, 128), vm(8, 24, 8, 128),
-                vm(16, 39, 8, 128), vm(8, 24, 8, 128),
+                vm(16, 51, 8, 128), vm(8, 24, 8, 128),
                 vm(CH, ATOMS), vm(4, 128, 128),
                 pltpu.VMEM((CH, 3 * HID), BF16), vm(CH, 128),
                 pltpu.VMEM((ATOMS, 128), BF16), pltpu.VMEM((8, 128), jnp.int32),
@@ -728,10 +734,10 @@
                 dma(4), dma(4), dma(4, 2), dma(4, 2),
             ],
             compiler_params=pltpu.CompilerParams(
-                collective_id=0, has_side_effects=True, vmem_limit_bytes=67_043_328
+                collective_id=0, has_side_effects=True, vmem_limit_bytes=48 * 1024 * 1024
             ),
-        )(*operands)
-        return jnp.transpose(out[0], (1, 0, 2))[None, None, None], out[1], out[2]
+        )(*(pltpu.with_memory_space_constraint(x, pltpu.HBM) for x in operands))
+        return jnp.transpose(out[0], (1, 0, 2))[None, None, None], out[1][:2], out[1][2:]
 
     return jax.shard_map(
         on_device,

time: 63.5 us -> 60.7 us (0.956)
  Pallas kernels: 60 us -> 58.6 us
  local copies, waits for them, and re-layouts: 2.58 us -> 1.2 us
    unnamed x7 -> x1, local copies, waits for them, and re-layouts: 2.58 us -> 0.6 us
    pallas_call x1, Pallas kernels: 60 us -> 58.6 us  [on_device(): pl.pallas_call(functools.partial(kernel, sizes), out_shape=(jax.ShapeDtyp...]
where the time goes in v4:
time: 60.7 us; the launch traced here: 60.5 us
  Pallas kernels  58.6 us (97%)
  local copies, waits for them, and re-layouts  1.2 us (2%)
  between operations  0.64 us (1%)
    pallas_call x1, Pallas kernels, on_device(): pl.pallas_call(functools.partial(kernel, sizes), out_shape=(jax.ShapeDtyp...  58.6 us

profile of v4, /device:TPU:1, one launch (start us, length us, event | category | flops | bytes accessed | tf_op | source)
XLA Modules:
  0.0 60.5 jit_solution(11163203403330879618)
XLA Ops:
  0.6 58.6 %shard_map.121 = (f32[3,4,256]{2,1,0:T(4,128)S(1)}, f32[4,4,4]{2,1,0:T(4,128)S(1)}) custom-call(f32[3,1,256]{2,1,0:T(1,128)} %bitcast.15, s32[1,256]{1,0:T(1,128)} %bitcast.16, f32[3,4,256]{2,1,0:T(4,128)} %bitcast.13, s32[6,1,256]{2,1,0:T(1,128)} %bitcast.14, s32[2,2,2,16]{3,2,1,0:T(2,128)} %refs_4_.1, f32[2,64]{1,0:T(2,128)} %refs_5_.1, f32[8,128]{1,0:T(8,128)} %refs_6_.1, ...), custom_call_target="tpu_custom_call" | custom-call | tf_op jit(solution)/shard_map/pallas_call | solution.py:708
  59.3 0.6 fusion
  59.9 0.6 copy.14

commit v5 on v4

--- a/solution.py
+++ b/solution.py
@@ -75,8 +75,12 @@
     return high, mid, low
 
 
+def stack(parts):
+    return jnp.concatenate([x.astype(F32) for x in parts], axis=0).astype(BF16)
+
+
 def rows3(x):
-    return jnp.concatenate(split3(x), axis=0)
+    return stack(split3(x))
 
 
 def sum3(y):
@@ -385,11 +389,16 @@
     def gather(src):
         got = sum3(mm(rows3(src), inc[...]))
         for k in range(FAN):
-            dt[:, k, :] = got[:, ATOMS * k : ATOMS * k + ATOMS]
+            for l in range(2):
+                at = ATOMS * k + 128 * l
+                dt[l, 16 * k : 16 * k + 16, :] = got[:, at : at + 128]
+
+    def edge(n):
+        return jnp.concatenate([dt[l, pl.ds(n, 8, stride=16), :] for l in range(2)], axis=1)
 
     gather(tab[...])
 
-    d3 = [dt[12 + h] for h in range(3)]
+    d3 = [edge(12 + h) for h in range(3)]
     dist2 = d3[0] * d3[0] + d3[1] * d3[1] + d3[2] * d3[2]
     dist = jnp.sqrt(dist2 + SOFTEN)
     inv_r = 1.0 / dist
@@ -398,7 +407,7 @@
         geo[h] = unit[h]
     geo[3] = dist
     geo[4] = inv_r
-    geo[5] = dt[15] + own[15:16, :]
+    geo[5] = edge(15) + own[15:16, :]
     for h in range(3):
         for k in range(FAN):
             row = jnp.broadcast_to(unit[h][k : k + 1, :], (8, ATOMS))
@@ -407,7 +416,7 @@
 
     def tangents(product):
         for v in range(4):
-            dv = [dt[4 * c + v] for c in range(3)]
+            dv = [edge(4 * c + v) for c in range(3)]
             rp = geo[0] * dv[0] + geo[1] * dv[1] + geo[2] * dv[2]
             parts = [rp] + [(dv[h] - geo[h] * rp) * geo[4] for h in range(3)]
             for g in range(4):
@@ -434,7 +443,7 @@
 
         def first(b):
             hi, mid, lo = split3(b)
-            return mm(rin_t, jnp.concatenate([hi, hi, hi, mid, mid, lo], axis=0))
+            return mm(rin_t, stack([hi, hi, hi, mid, mid, lo]))
 
         def second(h):
             hi = h.astype(BF16)
@@ -581,14 +590,14 @@
                 acc[vl, FAN * (h + 1) + k] += (dn[k] * e[h] + n[k] * de[h]) + f[k] * dq[h]
         return z
 
-    grs[12:16] = jnp.zeros((4, 8, ATOMS), F32)
+    grs[...] = jnp.zeros((2, 128, 128), F32)
 
     def finish_hvp():
         u3 = [geo[h] for h in hs]
         ir = geo[4]
         for v in range(4):
             got = fold(v)
-            dv = [dt[4 * c + v] for c in range(3)]
+            dv = [edge(4 * c + v) for c in range(3)]
             rp = u3[0] * dv[0] + u3[1] * dv[1] + u3[2] * dv[2]
             du = [(dv[h] - u3[h] * rp) * ir for h in hs]
             al, be, w0 = sums[0], sums[1], sums[2]
@@ -601,9 +610,10 @@
             for h in hs:
                 val = dal * u3[h] + al * du[h]
                 val = val + ir * ((dfo[h] - du[h] * w0 - u3[h] * duv) - back * (fo[h] - u3[h] * w0))
-                grs[4 * h + v] = val
+                for l in range(2):
+                    grs[l, pl.ds(4 * h + v, 8, stride=16), :] = val[:, 128 * l : 128 * l + 128]
         for k in ks:
-            cb[:, ATOMS * k : ATOMS * k + ATOMS] = rows3(grs[:, k, :])
+            cb[:, ATOMS * k : ATOMS * k + ATOMS] = rows3(jnp.concatenate([grs[l, 16 * k : 16 * k + 16, :] for l in range(2)], axis=1))
 
     def scatter(at):
         return sum3(mm(cb[...], inc_t[:, at]))
@@ -622,20 +632,31 @@
     def transposed(proj):
         return [place([proj[u][w] for w in range(4)]) for u in range(4)]
 
+    def less(gram, *projs):
+        out = [[None] * 4 for _ in range(4)]
+        for u in range(4):
+            for w in range(u + 1):
+                total = gram[u][w]
+                for proj in projs:
+                    for m in range(4):
+                        total = total - proj[m][u] * proj[m][w]
+                out[u][w] = total
+        return out
+
     clear()
     lax.fori_loop(0, 64, hvp, 0, unroll=2)
-    low, inv = cholesky(entries(ar_recv(0, 1), 0))
-    cols0 = columns_of(inv)
     local = give_back(1)
+    low, inv0 = cholesky(entries(ar_recv(0, 1), 0))
+    cols0 = columns_of(inv0)
     combine_all(v1, cols0, own)
-    w1[12:16, :] = jnp.zeros((4, ATOMS), F32)
     halo_wait(1)
     own[...] = local + unpack_back(1)
+    pack(2, own[...])
+    halo_send(2, -1)
     combine_all(w1, cols0, own)
-    pack(2, w1[...])
-    halo_send(2, -1)
-    ar_send(1, 0, jnp.concatenate([gram_rows(v1, w1), zeros4], axis=0))
-    tab[:, 0:256] = w1[...]
+    tile = gram_rows(v1, w1) + pltpu.roll(gram_rows(w1, w1), 4, 1)
+    ar_send(1, 0, jnp.concatenate([tile, zeros4], axis=0))
+    tab[:, 0:256] = own[...]
     clear()
     ar_send(1, 1, ar_recv(1, 0))
     halo_wait(2)
@@ -643,42 +664,40 @@
 
     gather(tab[...])
     tangents(1)
-    lax.fori_loop(0, 16, hvp, 0, unroll=2)
-    proj = entries(ar_recv(1, 1), 0)
-    cols_a = transposed(proj)
+    lax.fori_loop(0, 64, hvp, 0, unroll=2)
+    local = give_back(3)
+    tile = ar_recv(1, 1)
+    proj = entries(tile, 0)
+    low, inv = cholesky(less(entries(pltpu.roll(tile, 124, 1), 0), proj))
+    small_ref[0] = matrix(lambda u, w: proj[u][w])
+    small_ref[2] = matrix(lambda u, w: low[w][u] if w >= u else None)
+    cols1, cols_a = columns_of(inv), transposed(proj)
     combine_all(r1, cols_a, v1, w1)
-    ar_send(2, 0, jnp.concatenate([gram_rows(r1, r1), zeros4], axis=0))
-    small_ref[0] = matrix(lambda u, w: proj[u][w])
-    lax.fori_loop(16, 64, hvp, 0, unroll=2)
-    ar_send(2, 1, ar_recv(2, 0))
-    local = give_back(3)
-    low, inv = cholesky(entries(ar_recv(2, 1), 0))
-    cols1 = columns_of(inv)
-    small_ref[2] = matrix(lambda u, w: low[w][u] if w >= u else None)
     combine_all(v2, cols1, r1)
+    combine_all(r1, cols_a, w1)
+    combine_all(w1, cols1, r1)
+    both = [[None] * 4 for _ in range(4)]
+    for u in range(4):
+        for w in range(u + 1):
+            both[u][w] = sum((inv[u][m] * inv0[m][w] for m in range(w + 1, u + 1)), inv[u][w] * inv0[w][w])
+    cols01 = columns_of(both)
     for i in range(4):
         halo_all(i).wait_send()
-    for i in range(3):
+    for i in range(2):
         for g in range(2):
             ar_all(i, g).wait_send()
     halo_wait(3)
-    own[...] = local + unpack_back(3)
-    combine_all(r1, cols_a, w1, own)
-    combine_all(own, cols1, r1)
+    tab[:, 0:256] = local + unpack_back(3)
+    combine_all(own, cols01, tab.at[:, 0:256])
+    own[0:12, :] = own[0:12, :] - w1[0:12, :]
     gram_w = pltpu.roll(jnp.concatenate([gram_rows(own, own), zeros4], axis=0), 4, 1)
     tile = jnp.concatenate([gram_rows(v2, own), gram_rows(v1, own)], axis=0) + gram_w
     for g in range(2):
-        ar_send(3, g, tile)
-        tile = ar_recv(3, g)
+        ar_send(2, g, tile)
+        tile = ar_recv(2, g)
     proj = entries(tile, 0)
     prev = entries(tile, 4)
-    gram = entries(pltpu.roll(tile, 124, 1), 0)
-    for u in range(4):
-        for w in range(u + 1):
-            total = gram[u][w]
-            for m in range(4):
-                total = total - (proj[m][u] * proj[m][w] + prev[m][u] * prev[m][w])
-            gram[u][w] = total
+    gram = less(entries(pltpu.roll(tile, 124, 1), 0), proj, prev)
     combine_all(r1, transposed(proj), v2, own)
     combine_all(own, transposed(prev), v1, r1)
     low, inv = cholesky(gram)
@@ -688,7 +707,7 @@
     small_ref[1] = matrix(lambda u, w: proj[u][w])
     small_ref[3] = matrix(lambda u, w: low[w][u] if w >= u else None)
     for g in range(2):
-        ar_all(3, g).wait_send()
+        ar_all(2, g).wait_send()
 
 
 def solution(mesh):
@@ -721,7 +740,7 @@
                 pltpu.VMEM((FAN * ATOMS, COLS), BF16),
                 vm(ROWS, COLS),
                 vm(ROWS, ATOMS), vm(ROWS, ATOMS), vm(ROWS, ATOMS), vm(ROWS, ATOMS),
-                vm(ROWS, 8, ATOMS), vm(ROWS, 8, ATOMS),
+                vm(2, 128, 128), vm(2, 128, 128),
                 vm(6, 8, ATOMS), vm(9, 8, ATOMS),
                 vm(2, 18, 8, 128), vm(8, 24, 8, 128),
                 vm(16, 51, 8, 128), vm(8, 24, 8, 128),
@@ -730,8 +749,8 @@
                 pltpu.VMEM((ATOMS, 128), BF16), pltpu.VMEM((8, 128), jnp.int32),
                 pltpu.VMEM((3 * ROWS, FAN * ATOMS), BF16),
                 vm(4, GHOST, 256), vm(4, GHOST, 256),
-                vm(4, slots, 8, 128),
-                dma(4), dma(4), dma(4, 2), dma(4, 2),
+                vm(3, slots, 8, 128),
+                dma(4), dma(4), dma(3, 2), dma(3, 2),
             ],
             compiler_params=pltpu.CompilerParams(
                 collective_id=0, has_side_effects=True, vmem_limit_bytes=48 * 1024 * 1024

time: 60.7 us -> 58.5 us (0.964)
  Pallas kernels: 58.6 us -> 56.5 us
    pallas_call x1, Pallas kernels: 58.6 us -> 56.5 us  [on_device(): pl.pallas_call(functools.partial(kernel, sizes), out_shape=(jax.ShapeDtyp...]
where the time goes in v5:
time: 58.5 us; the launch traced here: 58.3 us
  Pallas kernels  56.5 us (97%)
  local copies, waits for them, and re-layouts  1.2 us (2%)
  between operations  0.64 us (1%)
    pallas_call x1, Pallas kernels, on_device(): pl.pallas_call(functools.partial(kernel, sizes), out_shape=(jax.ShapeDtyp...  56.5 us

profile of v5, /device:TPU:1, one launch (start us, length us, event | category | flops | bytes accessed | tf_op | source)
XLA Modules:
  0.0 58.3 jit_solution(254398056014620974)
XLA Ops:
  0.6 56.5 %shard_map.121 = (f32[3,4,256]{2,1,0:T(4,128)S(1)}, f32[4,4,4]{2,1,0:T(4,128)S(1)}) custom-call(f32[3,1,256]{2,1,0:T(1,128)} %bitcast.15, s32[1,256]{1,0:T(1,128)} %bitcast.16, f32[3,4,256]{2,1,0:T(4,128)} %bitcast.13, s32[6,1,256]{2,1,0:T(1,128)} %bitcast.14, s32[2,2,2,16]{3,2,1,0:T(2,128)} %refs_4_.1, f32[2,64]{1,0:T(2,128)} %refs_5_.1, f32[8,128]{1,0:T(8,128)} %refs_6_.1, ...), custom_call_target="tpu_custom_call" | custom-call | tf_op jit(solution)/shard_map/pallas_call | solution.py:727
  57.1 0.6 %fusion = (f32[2,4,4]{2,1,0:T(4,128)}, f32[2,4,4]{2,1,0:T(4,128)}) fusion(f32[4,4,4]{2,1,0:T(4,128)S(1)} %get-tuple-element.6), kind=kLoop, calls=%fused_computation | loop fusion | bytes 512 | tf_op jit(solution)/shard_map/slice | solution.py:759
  57.7 0.6 %copy.14 = f32[1,1,1,4,3,256]{5,3,4,2,1,0:T(4,128)} copy(f32[1,1,1,4,3,256]{5,3,4,2,1,0:T(4,128)S(1)} %bitcast.11) | data formatting | bytes 24576

commit v6 on v5

--- a/solution.py
+++ b/solution.py
@@ -644,7 +644,7 @@
         return out
 
     clear()
-    lax.fori_loop(0, 64, hvp, 0, unroll=2)
+    lax.fori_loop(0, 64, hvp, 0, unroll=4)
     local = give_back(1)
     low, inv0 = cholesky(entries(ar_recv(0, 1), 0))
     cols0 = columns_of(inv0)
@@ -664,7 +664,7 @@
 
     gather(tab[...])
     tangents(1)
-    lax.fori_loop(0, 64, hvp, 0, unroll=2)
+    lax.fori_loop(0, 64, hvp, 0, unroll=4)
     local = give_back(3)
     tile = ar_recv(1, 1)
     proj = entries(tile, 0)

time: 58.5 us -> 58.2 us (level)
  no operation moved by 1% of the time
where the time goes in v6:
time: 58.2 us; the launch traced here: 58 us
  Pallas kernels  56.2 us (97%)
  local copies, waits for them, and re-layouts  1.2 us (2%)
  between operations  0.64 us (1%)
    pallas_call x1, Pallas kernels, on_device(): pl.pallas_call(functools.partial(kernel, sizes), out_shape=(jax.ShapeDtyp...  56.2 us

profile of v6, /device:TPU:1, one launch (start us, length us, event | category | flops | bytes accessed | tf_op | source)
XLA Modules:
  0.0 58.0 jit_solution(3720070770940788230)
XLA Ops:
  0.6 56.2 %shard_map.121 = (f32[3,4,256]{2,1,0:T(4,128)S(1)}, f32[4,4,4]{2,1,0:T(4,128)S(1)}) custom-call(f32[3,1,256]{2,1,0:T(1,128)} %bitcast.15, s32[1,256]{1,0:T(1,128)} %bitcast.16, f32[3,4,256]{2,1,0:T(4,128)} %bitcast.13, s32[6,1,256]{2,1,0:T(1,128)} %bitcast.14, s32[2,2,2,16]{3,2,1,0:T(2,128)} %refs_4_.1, f32[2,64]{1,0:T(2,128)} %refs_5_.1, f32[8,128]{1,0:T(8,128)} %refs_6_.1, ...), custom_call_target="tpu_custom_call" | custom-call | tf_op jit(solution)/shard_map/pallas_call | solution.py:727
  56.8 0.6 %fusion = (f32[2,4,4]{2,1,0:T(4,128)}, f32[2,4,4]{2,1,0:T(4,128)}) fusion(f32[4,4,4]{2,1,0:T(4,128)S(1)} %get-tuple-element.6), kind=kLoop, calls=%fused_computation | loop fusion | bytes 512 | tf_op jit(solution)/shard_map/slice | solution.py:759
  57.4 0.6 %copy.14 = f32[1,1,1,4,3,256]{5,3,4,2,1,0:T(4,128)} copy(f32[1,1,1,4,3,256]{5,3,4,2,1,0:T(4,128)S(1)} %bitcast.11) | data formatting | bytes 24576
